TPU v7x, 32 devices: a whole 2x2x4 slice. The times are simulated.
32 devices in a mesh: angle: 2 (over y), tile: 8 (over z, core), layer: 2 (over x).
Axes of the slice: x: 2, y: 2, z: 4, core: 2. Of those that a mesh axis runs over, the one named last changes fastest.
Arguments:
- frames: bfloat16 [2, 1024, 192, 512], P('layer', 'angle', 'tile'), may hold values from 0.0625 to 8, as said below
- exponents: int32 [2, 1024, 192, 4], P('layer', 'angle', 'tile'), may hold values from -1 to 1
- valid_mask: int32 [2, 192, 512], P('layer', 'tile', 'angle'), may hold values 0 or 1
Outputs:
- orientation: float32 [2, 2, 192, 512], P(None, 'layer', 'tile', 'angle')
- spread: float32 [3, 2, 192, 512], P(None, 'layer', 'tile', 'angle')
- nye_tensor: float32 [7, 2, 192, 512], P(None, 'layer', 'tile', 'angle')
Inputs may be any that keep to these rules, and one draw needn't show every extreme that they name: `frames`: positive intensities.
All inputs are finite; a program needn't handle non-finite values. No bound on the sum of `valid_mask` on one device may be relied on, other than what follows from the above.
Results may differ from a plain program's by a relative error of at most 0.0003.
Values sent between devices are 32-bit elements; how exact they have to be, the bound alone decides.
No kernel may reach another device: no remote copies, remote signals or barrier semaphores. Data moves between devices by JAX's collectives and lax.ppermute only.
A program may use at most 128 MiB of HBM per device.

v0:
```python
import jax
import jax.numpy as jnp
from jax import lax
from jax.sharding import PartitionSpec as P

NPHI = 32
NCHI = 32


layer_pitch = 2.0


def padded_2(cells, sides, width):
    for axis, dim in sides:
        count = lax.axis_size(axis)
        ends = count - 1
        head = lax.slice_in_dim(cells, 0, width, axis=dim)
        tail = lax.slice_in_dim(cells, cells.shape[dim] - width, cells.shape[dim], axis=dim)
        cells = jnp.concatenate(
            [
                lax.ppermute(tail, axis, [(i, (i + 1) % count) for i in range(ends)]),
                cells,
                lax.ppermute(head, axis, [((i + 1) % count, i) for i in range(ends)]),
            ],
            axis=dim,
        )
    return cells


def angle_table(first_angle, count_angles):
    position = first_angle + jnp.arange(count_angles, dtype=jnp.int32)
    phi_index = (position // NCHI).astype(jnp.float32)
    chi_index = (position % NCHI).astype(jnp.float32)
    phi_coord = (phi_index - 0.5 * (NPHI - 1)) / (0.5 * NPHI)
    chi_coord = (chi_index - 0.5 * (NCHI - 1)) / (0.5 * NCHI)
    constant = jnp.ones_like(phi_coord)
    return jnp.stack(
        [
            constant,
            phi_coord,
            chi_coord,
            phi_coord * phi_coord,
            chi_coord * chi_coord,
            phi_coord * chi_coord,
        ]
    ).astype(jnp.bfloat16)


def intensity_of(frames, exponents):
    layers_here, angles_here, rows_here, columns = frames.shape
    blocks = exponents.shape[3]
    factor = jnp.exp2(exponents.astype(jnp.float32)).astype(jnp.bfloat16)
    scaled = (
        frames.reshape(layers_here, angles_here, rows_here, blocks, columns // blocks)
        * factor[..., None]
    )
    return scaled.reshape(layers_here, angles_here, rows_here * columns)


def orientation_of(moments):
    zeroth = moments[0]
    return jnp.stack([moments[1] / zeroth, moments[2] / zeroth])


def spread_of(moments, orient):
    zeroth = moments[0]
    return jnp.stack(
        [
            moments[3] / zeroth - orient[0] * orient[0],
            moments[4] / zeroth - orient[1] * orient[1],
            moments[5] / zeroth - orient[0] * orient[1],
        ]
    )


def nye_of(padded):
    along_x = 0.5 * (padded[:, 1:-1, 1:-1, 2:] - padded[:, 1:-1, 1:-1, :-2])
    along_y = 0.5 * (padded[:, 1:-1, 2:, 1:-1] - padded[:, 1:-1, :-2, 1:-1])
    along_z = 0.5 / layer_pitch * (padded[:, 2:, 1:-1, 1:-1] - padded[:, :-2, 1:-1, 1:-1])
    trace_sum = along_x[0] + along_y[1]
    return jnp.stack(
        [-along_y[1], -along_x[0], -trace_sum, along_x[1], along_y[0], along_z[0], along_z[1]]
    )


def on_device(frames, exponents, valid_mask):
    layers_here, angles_here, rows_here, columns = frames.shape
    intensity = intensity_of(frames, exponents)
    angle_weights = angle_table(lax.axis_index("angle") * angles_here, angles_here)
    partial_value = jnp.einsum(
        "ma,lax->mlx", angle_weights, intensity, preferred_element_type=jnp.float32
    )
    partial_value = partial_value.reshape(6, layers_here, rows_here, columns)
    moments = lax.psum_scatter(partial_value, "angle", scatter_dimension=3, tiled=True)
    orient = orientation_of(moments)
    padded = padded_2(orient, (("angle", 3), ("tile", 2), ("layer", 1)), 1)
    mask_float = valid_mask.astype(jnp.float32)
    spread = spread_of(moments, orient) * mask_float
    nye_tensor = nye_of(padded) * mask_float
    return (orient * mask_float, spread, nye_tensor)


def solution(mesh):
    in_specs = (
        P("layer", "angle", "tile", None),
        P("layer", "angle", "tile", None),
        P("layer", "tile", "angle"),
    )
    out_specs = (
        P(None, "layer", "tile", "angle"),
        P(None, "layer", "tile", "angle"),
        P(None, "layer", "tile", "angle"),
    )
    return jax.shard_map(
        on_device, mesh=mesh, in_specs=in_specs, out_specs=out_specs, check_vma=False
    )
```

profile of v0, /device:TPU:1, one launch (start us, length us, event | category | flops | bytes accessed | tf_op | source)
XLA Modules:
  0.0 133.2 jit_solution(4052266713521713430)
XLA Ops:
  7.2 0.0 reduce-scatter.2.cloned.1.call-start
  7.3 1.0 fusion
  8.3 2.6 %copy.11 = bf16[512,24,4]{2,1,0:T(8,128)(2,1)S(1)} copy(bf16[512,24,4]{0,2,1:T(4,128)(2,1)S(1)} %fusion) | data formatting | bytes 196608 | tf_op jit(solution)/shard_map/mul | solution.py:54
  10.9 15.9 %mul.134 = bf16[512,24,4,128]{3,2,1,0:T(4,128)(2,1)} broadcast(bf16[512,24,4]{2,1,0:T(8,128)(2,1)S(1)} %copy.11), dimensions={0,1,2} | broadcast | bytes 12681216 | tf_op jit(solution)/shard_map/mul | solution.py:54
  26.7 20.7 %mul.135 = bf16[512,12288]{1,0:T(8,128)(2,1)} reshape(bf16[512,24,4,128]{3,2,1,0:T(4,128)(2,1)} %mul.134) | data formatting | bytes 25165824 | tf_op jit(solution)/shard_map/mul | solution.py:54
  47.4 0.0 copy-start
  47.4 10.0 %copy.14 = bf16[64,8,24,512]{3,1,2,0:T(8,128)(2,1)S(1)} copy(bf16[64,8,24,512]{3,2,1,0:T(8,128)(2,1)} %bitcast.19) | data formatting | bytes 25165824
  57.5 0.0 copy-done
  57.5 5.6 %multiply_bitcast_fusion = bf16[12288,512]{0,1:T(8,128)(2,1)} fusion(bf16[512,12288]{1,0:T(8,128)(2,1)S(1)} %bitcast.18, bf16[512,12288]{1,0:T(8,128)(2,1)S(1)} %copy-done), kind=kLoop, calls=%fused_computation | loop fusion | flops 6291456 | bytes 37748736 | tf_op jit(solution)/shard_map/ma,lax->mlx/dot_general | solution.py:90
  63.1 15.7 %copy.12 = bf16[12288,512]{1,0:T(8,128)(2,1)} copy(bf16[12288,512]{0,1:T(8,128)(2,1)} %multiply_bitcast_fusion) | data formatting | bytes 25165824 | tf_op jit(solution)/shard_map/ma,lax->mlx/dot_general | solution.py:90
  78.8 0.0 copy-start.1
  78.9 7.9 %fusion.13 = f32[6,24,512]{2,0,1:T(8,128)S(1)} fusion(bf16[24,512,512]{2,1,0:T(8,128)(2,1)} %bitcast.17, bf16[6,512]{1,0:T(8,128)(2,1)S(1)} %stack.10), kind=kOutput, calls=%fused_computation.48 | convolution fusion | flops 75497472 | bytes 12883968 | tf_op jit(solution)/shard_map/ma,lax->mlx/dot_general | solution.py:90
  86.8 0.9 copy.16
  87.7 0.0 reduce-scatter.2.cloned.1.call-update
  87.7 0.0 copy-done.1
  87.7 14.2 %reduce-scatter.2.cloned.1.call-done = f32[6,1,24,256]{3,2,1,0:T(8,128)} async-done(((f32[6,1,24,512]{3,2,1,0:T(8,128)}), f32[6,1,24,256]{3,2,1,0:T(8,128)}) %reduce-scatter.2.cloned.1.call-update) | async-done | bytes 147472 | tf_op jit(solution)/shard_map/reduce_scatter | solution.py:94
  101.9 0.8 fusion.12
  102.7 0.1 fusion.8
  102.8 2.1 %collective-permute-start = (f32[2,1,24,1]{3,2,1,0:T(8,128)S(1)}, f32[2,1,24,1]{3,2,1,0:T(8,128)S(1)}, u32[]{:S(2)}, u32[]{:S(2)}) collective-permute-start(f32[2,1,24,1]{3,2,1,0:T(8,128)S(1)} %get-tuple-element.17), channel_id=1, source_target_pairs={{0,16},{1,17},{2,18},{3,19},{4,20},{5,21},{6,22},{7,23},{8,24},{9,... | collective-permute-start | bytes 584 | tf_op jit(solution)/shard_map/ppermute | solution.py:21
  104.9 1.3 collective-permute-start.1
  106.2 0.8 fusion.10
  107.0 0.0 collective-permute-done
  107.0 2.5 %collective-permute-done.1 = f32[2,1,24,1]{3,2,1,0:T(8,128)S(1)} collective-permute-done((f32[2,1,24,1]{3,2,1,0:T(8,128)S(1)}, f32[2,1,24,1]{3,2,1,0:T(8,128)S(1)}, u32[]{:S(2)}, u32[]{:S(2)}) %collective-permute-start.1) | collective-permute-done | bytes 224 | tf_op jit(solution)/shard_map/ppermute | solution.py:23
  109.5 0.1 pad_maximum_fusion.17
  109.6 4.0 %collective-permute-start.2 = (f32[2,1,1,258]{3,2,1,0:T(1,128)S(1)}, f32[2,1,1,258]{3,2,1,0:T(1,128)S(1)}, u32[]{:S(2)}, u32[]{:S(2)}) collective-permute-start(f32[2,1,1,258]{3,2,1,0:T(1,128)S(1)} %get-tuple-element.14), channel_id=1, source_target_pairs={{2,0},{4,2},{6,4},{8,6},{10,8},{12,10},{14,12},{3,1},{5,3},{7,5},{... | collective-permute-start | bytes 6200 | tf_op jit(solution)/shard_map/ppermute | solution.py:23
  113.6 3.2 %collective-permute-start.3 = (f32[2,1,1,258]{3,2,1,0:T(1,128)S(1)}, f32[2,1,1,258]{3,2,1,0:T(1,128)S(1)}, u32[]{:S(2)}, u32[]{:S(2)}) collective-permute-start(f32[2,1,1,258]{3,2,1,0:T(1,128)S(1)} %get-tuple-element.15), channel_id=1, source_target_pairs={{0,2},{2,4},{4,6},{6,8},{8,10},{10,12},{12,14},{1,3},{3,5},{5,7},{... | collective-permute-start | bytes 6200 | tf_op jit(solution)/shard_map/ppermute | solution.py:21
  116.8 0.6 maximum_multiply_fusion
  117.5 0.0 collective-permute-done.2
  117.5 0.1 collective-permute-done.3
  117.5 0.1 pad_maximum_fusion
  117.6 1.3 collective-permute-start.4
  118.9 4.0 %collective-permute-start.5 = (f32[2,1,26,258]{3,2,1,0:T(8,128)S(1)}, f32[2,1,26,258]{3,2,1,0:T(8,128)S(1)}, u32[]{:S(2)}, u32[]{:S(2)}) collective-permute-start(f32[2,1,26,258]{3,2,1,0:T(8,128)S(1)} %pad_maximum_fusion), channel_id=1, source_target_pairs={{0,1},{2,3},{4,5},{6,7},{8,9},{10,11},{12,13},{14,15},{16,17},{18,... | collective-permute-start | bytes 161000 | tf_op jit(solution)/shard_map/ppermute | solution.py:21
  122.9 0.7 fusion.5
  123.7 0.1 collective-permute-done.4
  123.8 1.8 %collective-permute-done.5 = f32[2,1,26,258]{3,2,1,0:T(8,128)S(1)} collective-permute-done((f32[2,1,26,258]{3,2,1,0:T(8,128)S(1)}, f32[2,1,26,258]{3,2,1,0:T(8,128)S(1)}, u32[]{:S(2)}, u32[]{:S(2)}) %collective-permute-start.5) | collective-permute-done | bytes 53696 | tf_op jit(solution)/shard_map/ppermute | solution.py:21
  125.5 0.1 fusion.3
  125.6 0.7 broadcast_multiply_fusion
  (11 shorter events, 0.1 us)
Async XLA Ops:
  7.2 94.7 %reduce-scatter.2.cloned.1.call-start = ((), (), s32[]{:S(2)}) async-start(), calls=%async_computation.1 | async-start | bytes 442368 | tf_op jit(solution)/shard_map/reduce_scatter | solution.py:94
  47.4 10.1 %copy-start = (bf16[512,12288]{1,0:T(8,128)(2,1)S(1)}, bf16[512,12288]{1,0:T(8,128)(2,1)}, u32[]{:S(2)}) copy-start(bf16[512,12288]{1,0:T(8,128)(2,1)} %mul.135) | copy-start | bytes 37748740
  78.8 8.9 %copy-start.1 = (s32[1,24,256]{2,1,0:T(8,128)S(1)}, s32[1,24,256]{2,1,0:T(8,128)}, u32[]{:S(2)}) copy-start(s32[1,24,256]{2,1,0:T(8,128)} %param.5) | copy-start | bytes 73732
  102.8 4.2 %collective-permute-start = (f32[2,1,24,1]{3,2,1,0:T(8,128)S(1)}, f32[2,1,24,1]{3,2,1,0:T(8,128)S(1)}, u32[]{:S(2)}, u32[]{:S(2)}) collective-permute-start(f32[2,1,24,1]{3,2,1,0:T(8,128)S(1)} %get-tuple-element.17), channel_id=1, source_target_pairs={{0,16},{1,17},{2,18},{3,19},{4,20},{5,21},{6,22},{7,23},{8,24},{9,... | collective-permute-start | bytes 584 | tf_op jit(solution)/shard_map/ppermute | solution.py:21
  104.9 4.6 %collective-permute-start.1 = (f32[2,1,24,1]{3,2,1,0:T(8,128)S(1)}, f32[2,1,24,1]{3,2,1,0:T(8,128)S(1)}, u32[]{:S(2)}, u32[]{:S(2)}) collective-permute-start(f32[2,1,24,1]{3,2,1,0:T(8,128)S(1)} %get-tuple-element.18), channel_id=1, source_target_pairs={{16,0},{17,1},{18,2},{19,3},{20,4},{21,5},{22,6},{23,7},{24,8},{25... | collective-permute-start | bytes 584 | tf_op jit(solution)/shard_map/ppermute | solution.py:23
  109.6 7.9 %collective-permute-start.2 = (f32[2,1,1,258]{3,2,1,0:T(1,128)S(1)}, f32[2,1,1,258]{3,2,1,0:T(1,128)S(1)}, u32[]{:S(2)}, u32[]{:S(2)}) collective-permute-start(f32[2,1,1,258]{3,2,1,0:T(1,128)S(1)} %get-tuple-element.14), channel_id=1, source_target_pairs={{2,0},{4,2},{6,4},{8,6},{10,8},{12,10},{14,12},{3,1},{5,3},{7,5},{... | collective-permute-start | bytes 6200 | tf_op jit(solution)/shard_map/ppermute | solution.py:23
  113.6 4.0 %collective-permute-start.3 = (f32[2,1,1,258]{3,2,1,0:T(1,128)S(1)}, f32[2,1,1,258]{3,2,1,0:T(1,128)S(1)}, u32[]{:S(2)}, u32[]{:S(2)}) collective-permute-start(f32[2,1,1,258]{3,2,1,0:T(1,128)S(1)} %get-tuple-element.15), channel_id=1, source_target_pairs={{0,2},{2,4},{4,6},{6,8},{8,10},{10,12},{12,14},{1,3},{3,5},{5,7},{... | collective-permute-start | bytes 6200 | tf_op jit(solution)/shard_map/ppermute | solution.py:21
  117.6 6.1 %collective-permute-start.4 = (f32[2,1,26,258]{3,2,1,0:T(8,128)S(1)}, f32[2,1,26,258]{3,2,1,0:T(8,128)S(1)}, u32[]{:S(2)}, u32[]{:S(2)}) collective-permute-start(f32[2,1,26,258]{3,2,1,0:T(8,128)S(1)} %pad_maximum_fusion), channel_id=1, source_target_pairs={{1,0},{3,2},{5,4},{7,6},{9,8},{11,10},{13,12},{15,14},{17,16},{19,... | collective-permute-start | bytes 161000 | tf_op jit(solution)/shard_map/ppermute | solution.py:23
  118.9 6.6 %collective-permute-start.5 = (f32[2,1,26,258]{3,2,1,0:T(8,128)S(1)}, f32[2,1,26,258]{3,2,1,0:T(8,128)S(1)}, u32[]{:S(2)}, u32[]{:S(2)}) collective-permute-start(f32[2,1,26,258]{3,2,1,0:T(8,128)S(1)} %pad_maximum_fusion), channel_id=1, source_target_pairs={{0,1},{2,3},{4,5},{6,7},{8,9},{10,11},{12,13},{14,15},{16,17},{18,... | collective-permute-start | bytes 161000 | tf_op jit(solution)/shard_map/ppermute | solution.py:21
Sparse Core Ops, SparseCore 0:
  87.8 14.0 reduce-scatter.1
where the time goes:
time: 135 us; the launch traced here: 133 us
  local copies, waits for them, and re-layouts  65.8 us (49%)
  waiting for transfers between devices  18.6 us (14%)
  starting transfers between devices  16 us (12%)
  between operations  14.2 us (11%)
  other arithmetic  10.6 us (8%)
  matrix products  7.9 us (6%)
    mul x3, local copies, waits for them, and re-layouts, intensity_of(): frames.reshape(layers_here, angles_here, rows_here, blocks, columns // bl...  39.1 us
    dot_general x2, local copies, waits for them, and re-layouts, on_device(): jnp.einsum('ma,lax->mlx', angle_weights, intensity, preferred_element_typ...  16.6 us
    reduce_scatter x1, waiting for transfers between devices, on_device(): lax.psum_scatter(partial_value, 'angle', scatter_dimension=3, tiled=True)  14.2 us
    unnamed x7, local copies, waits for them, and re-layouts  10.1 us
    ppermute x3, starting transfers between devices, padded_2(): lax.ppermute(tail, axis, [(i, (i + 1) % count) for i in range(ends)])  9.37 us
    dot_general x1, matrix products, on_device(): jnp.einsum('ma,lax->mlx', angle_weights, intensity, preferred_element_typ...  7.9 us
    ppermute x3, starting transfers between devices, padded_2(): lax.ppermute(head, axis, [((i + 1) % count, i) for i in range(ends)])  6.57 us
    dot_general x1, other arithmetic, on_device(): jnp.einsum('ma,lax->mlx', angle_weights, intensity, preferred_element_typ...  5.58 us
  transfers between devices with their start and end apart: 7, of which 5 were waited for; matrix products, arithmetic and copies ran while one was open for 2% of the time, Pallas kernels for 0%

commit v1 on v0

v1 whole, which is shorter than its diff:
```python
import functools
import jax
import jax.numpy as jnp
from jax import lax
from jax.experimental import pallas as pl
from jax.experimental.pallas import tpu as pltpu
from jax.sharding import PartitionSpec as P

NPHI = 32
NCHI = 32
layer_pitch = 2.0
F32 = jnp.float32
BF16 = jnp.bfloat16
VMEM = pl.BlockSpec(memory_space=pltpu.VMEM)
ANY = pl.BlockSpec(memory_space=pl.ANY)


def moments_body(shift, count, steps, e_hbm, f_hbm, low_ref, high_ref, buf, ebuf, sem, esem):
    angles, rows, width = buf.shape
    blocks = ebuf.shape[1]
    span = f_hbm.shape[2] // blocks
    here = width // span
    deep = NCHI * 8
    me = lax.axis_index("angle")
    block = lax.rem(me + shift, count)
    column = pl.multiple_of(block * width, width)
    exponent_copy = pltpu.make_async_copy(e_hbm, ebuf, esem)
    exponent_copy.start()
    size = angles // steps
    copies = []
    for step in range(steps):
        part = pl.ds(step * size, size)
        copy = pltpu.make_async_copy(
            f_hbm.at[part, :, pl.ds(column, width)], buf.at[part], sem.at[step]
        )
        copy.start()
        copies.append(copy)
    low_ref[...] = jnp.zeros_like(low_ref)
    high_ref[...] = jnp.zeros_like(high_ref)
    lane = lax.broadcasted_iota(jnp.int32, (8, deep), 1)
    diagonal = (lane & 7) == lax.broadcasted_iota(jnp.int32, (8, deep), 0)
    chi = ((lane >> 3).astype(F32) - 0.5 * (NCHI - 1)) / (0.5 * NCHI)
    chi_chi = (chi * chi).astype(BF16).astype(F32)
    source = lax.broadcasted_iota(jnp.int32, (128, deep), 0)
    target = lax.broadcasted_iota(jnp.int32, (128, deep), 1) >> 3
    spread_out = [
        (source == target + NCHI * part).astype(F32).astype(BF16) for part in range(128 // NCHI)
    ]
    exponent_copy.wait()
    factor = jnp.concatenate(
        [
            jnp.exp2(ebuf[:, pl.ds(block * here + b, 1), :].reshape(rows, angles).astype(F32))
            for b in range(here)
        ],
        0,
    ).astype(BF16)
    first_phi = me * (angles // NCHI)
    for g in range(angles // NCHI):
        if (g * NCHI) % size == 0:
            copies[(g * NCHI) // size].wait()
        chunk = g * NCHI // 128 * 128
        factors = jnp.dot(
            factor[:, chunk : chunk + 128],
            spread_out[g % (128 // NCHI)],
            preferred_element_type=F32,
        )
        phi = ((first_phi + g).astype(F32) - 0.5 * (NPHI - 1)) / (0.5 * NPHI)
        phi_chi = (phi * chi).astype(BF16).astype(F32)
        phi_phi = jnp.full((8, 128), phi * phi, F32).astype(BF16).astype(F32)[:, :1]
        for r in range(rows // 8):
            at_rows = slice(r * 8, r * 8 + 8)
            for b in range(here):
                at_columns = slice(b * span, (b + 1) * span)
                top = b * rows + r * 8
                unit = jnp.where(diagonal, factors[top : top + 8], 0.0)
                left = jnp.concatenate([unit, unit * chi, unit * chi_chi, unit * phi_chi], 0)
                cells = buf[g * NCHI : (g + 1) * NCHI, at_rows, at_columns].reshape(deep, span)
                sums = jnp.dot(left.astype(BF16), cells, preferred_element_type=F32)
                low_ref[0, at_rows, at_columns] += sums[:8]
                low_ref[1, at_rows, at_columns] += sums[:8] * phi
                low_ref[2, at_rows, at_columns] += sums[8:16]
                high_ref[0, at_rows, at_columns] += sums[:8] * phi_phi
                high_ref[1, at_rows, at_columns] += sums[16:24]
                high_ref[2, at_rows, at_columns] += sums[24:]


def partial_moments(frames, exponents, shift, count):
    angles, rows, columns = frames.shape
    width = columns // count
    steps = 8
    return pl.pallas_call(
        functools.partial(moments_body, shift, count, steps),
        out_shape=[jax.ShapeDtypeStruct((3, rows, width), F32)] * 2,
        in_specs=[ANY, ANY],
        out_specs=[VMEM, VMEM],
        scratch_shapes=[
            pltpu.VMEM((angles, rows, width), BF16),
            pltpu.VMEM(exponents.shape, jnp.int32),
            pltpu.SemaphoreType.DMA((steps,)),
            pltpu.SemaphoreType.DMA,
        ],
        name=f"moments_{shift}",
        cost_estimate=pl.CostEstimate(
            flops=512 * angles * rows * width,
            bytes_accessed=2 * angles * rows * width,
            transcendentals=0,
        ),
    )(exponents, frames)


def field_body(count, own_ref, *refs):
    parts, (field_ref, even_ref, odd_ref) = refs[: count - 1], refs[count - 1 :]
    total = own_ref[...]
    for part in parts:
        total = total + part[...]
    first = total[1] / total[0]
    second = total[2] / total[0]
    field_ref[0] = first
    field_ref[1] = second
    rows = first.shape[0]
    is_even = lax.rem(lax.axis_index("tile"), 2) == 0
    for c, value in ((0, first), (1, second)):
        head, tail = value[:1], value[rows - 1 :]
        even_ref[c] = jnp.where(is_even, tail, head)
        odd_ref[c] = jnp.where(is_even, head, tail)


def field_of(own, parts):
    _, rows, width = own.shape
    edge = jax.ShapeDtypeStruct((2, 1, width), F32)
    return pl.pallas_call(
        functools.partial(field_body, len(parts) + 1),
        out_shape=[jax.ShapeDtypeStruct((2, rows, width), F32), edge, edge],
        in_specs=[VMEM] * (len(parts) + 1),
        out_specs=[VMEM] * 3,
        name="field",
    )(own, *parts)


def spread_body(count, mask_ref, field_ref, low_ref, high_ref, *refs):
    parts, (orient_ref, spread_ref) = refs[: 2 * count - 2], refs[2 * count - 2 :]
    mask = mask_ref[0].astype(F32)
    zeroth = low_ref[0]
    seconds = high_ref[...]
    for k in range(count - 1):
        zeroth = zeroth + parts[2 * k][0]
        seconds = seconds + parts[2 * k + 1][...]
    first, second = field_ref[0], field_ref[1]
    orient_ref[0, 0] = first * mask
    orient_ref[1, 0] = second * mask
    spread_ref[0, 0] = (seconds[0] / zeroth - first * first) * mask
    spread_ref[1, 0] = (seconds[1] / zeroth - second * second) * mask
    spread_ref[2, 0] = (seconds[2] / zeroth - first * second) * mask


def spread_of(mask, field, low, high, parts):
    _, rows, width = field.shape
    flat = [x for pair in parts for x in pair]
    return pl.pallas_call(
        functools.partial(spread_body, len(parts) + 1),
        out_shape=[
            jax.ShapeDtypeStruct((2, 1, rows, width), F32),
            jax.ShapeDtypeStruct((3, 1, rows, width), F32),
        ],
        in_specs=[VMEM] * (4 + len(flat)),
        out_specs=[VMEM] * 2,
        name="spread",
    )(mask, field, low, high, *flat)


def nye_body(mask_ref, field_ref, even_ref, odd_ref, left_ref, right_ref, below_ref, above_ref, nye_ref):
    rows, width = field_ref.shape[1:]
    mask = mask_ref[0].astype(F32)
    is_even = lax.rem(lax.axis_index("tile"), 2) == 0
    row = lax.broadcasted_iota(jnp.int32, (rows, width), 0)
    column = lax.broadcasted_iota(jnp.int32, (rows, width), 1)
    along_x, along_y, along_z = [], [], []
    for c in range(2):
        value = field_ref[c]
        upper = jnp.where(is_even, odd_ref[c], even_ref[c])
        lower = jnp.where(is_even, even_ref[c], odd_ref[c])
        before = jnp.where(row == 0, upper, pltpu.roll(value, 1, 0))
        after = jnp.where(row == rows - 1, lower, pltpu.roll(value, rows - 1, 0))
        along_y.append(0.5 * (after - before))
        before = jnp.where(column == 0, left_ref[c], pltpu.roll(value, 1, 1))
        after = jnp.where(column == width - 1, right_ref[c], pltpu.roll(value, width - 1, 1))
        along_x.append(0.5 * (after - before))
        along_z.append((0.5 / layer_pitch) * (above_ref[c] - below_ref[c]))
    nye_ref[0, 0] = -along_y[1] * mask
    nye_ref[1, 0] = -along_x[0] * mask
    nye_ref[2, 0] = -(along_x[0] + along_y[1]) * mask
    nye_ref[3, 0] = along_x[1] * mask
    nye_ref[4, 0] = along_y[0] * mask
    nye_ref[5, 0] = along_z[0] * mask
    nye_ref[6, 0] = along_z[1] * mask


def nye_of(mask, field, even, odd, left, right, below, above):
    _, rows, width = field.shape
    return pl.pallas_call(
        nye_body,
        out_shape=jax.ShapeDtypeStruct((7, 1, rows, width), F32),
        in_specs=[VMEM] * 8,
        out_specs=VMEM,
        name="nye",
    )(mask, field, even, odd, left, right, below, above)


def swap_pairs(count, start):
    pairs = []
    for i in range(start, count - 1, 2):
        pairs += [(i, i + 1), (i + 1, i)]
    return pairs


def both_sides(tail, head, axis):
    count = lax.axis_size(axis)
    return (
        lax.ppermute(tail, axis, [(i, i + 1) for i in range(count - 1)]),
        lax.ppermute(head, axis, [(i + 1, i) for i in range(count - 1)]),
    )


def on_device(frames, exponents, valid_mask):
    count = lax.axis_size("angle")
    frames = frames[0]
    exponents = exponents[0].transpose(1, 2, 0)
    sent = []
    for shift in range(1, count):
        low, high = partial_moments(frames, exponents, shift, count)
        pairs = [(i, (i + shift) % count) for i in range(count)]
        sent.append((lax.ppermute(low, "angle", pairs), lax.ppermute(high, "angle", pairs)))
    low, high = partial_moments(frames, exponents, 0, count)
    field, even, odd = field_of(low, [part[0] for part in sent])
    below, above = both_sides(field, field, "layer")
    tiles = lax.axis_size("tile")
    even = lax.ppermute(even, "tile", swap_pairs(tiles, 0))
    odd = lax.ppermute(odd, "tile", swap_pairs(tiles, 1))
    left, right = both_sides(field[:, :, -1:], field[:, :, :1], "angle")
    orient, spread = spread_of(valid_mask, field, low, high, sent)
    nye = nye_of(valid_mask, field, even, odd, left, right, below, above)
    return orient, spread, nye


def solution(mesh):
    in_specs = (
        P("layer", "angle", "tile", None),
        P("layer", "angle", "tile", None),
        P("layer", "tile", "angle"),
    )
    out_specs = (P(None, "layer", "tile", "angle"),) * 3
    return jax.shard_map(
        on_device, mesh=mesh, in_specs=in_specs, out_specs=out_specs, check_vma=False
    )
```

time: 135 us -> 40.5 us (0.30); the launches traced: 133 us -> 40.1 us
  local copies, waits for them, and re-layouts: 65.8 us -> 2.65 us
  Pallas kernels: 0 us -> 17.8 us
  waiting for transfers between devices: 18.6 us -> 3.29 us
  between operations: 14.2 us -> 0.78 us
  other arithmetic: 10.6 us -> 0 us
  matrix products: 7.9 us -> 0 us
    mul x3 -> x0, local copies, waits for them, and re-layouts: 39.1 us -> none  [intensity_of(): frames.reshape(layers_here, angles_here, rows_here, blocks, columns // bl...]
    pallas_call x0 -> x5, Pallas kernels: none -> 17.8 us  [the longest x2 12.9 us: partial_moments(): pl.pallas_call(functools.partial(moments_body, shift, count, steps), out_...]
    dot_general x2 -> x0, local copies, waits for them, and re-layouts: 16.6 us -> none  [on_device(): jnp.einsum('ma,lax->mlx', angle_weights, intensity, preferred_element_typ...]
    reduce_scatter x1 -> x0, waiting for transfers between devices: 14.2 us -> none  [on_device(): lax.psum_scatter(partial_value, 'angle', scatter_dimension=3, tiled=True)]
    unnamed x7 -> x16, local copies, waits for them, and re-layouts: 10.1 us -> 1.82 us
    dot_general x1 -> x0, matrix products: 7.9 us -> none  [on_device(): jnp.einsum('ma,lax->mlx', angle_weights, intensity, preferred_element_typ...]
    dot_general x1 -> x0, other arithmetic: 5.58 us -> none  [on_device(): jnp.einsum('ma,lax->mlx', angle_weights, intensity, preferred_element_typ...]
    mul x5 -> x0, other arithmetic: 3 us -> none  [the longest x1 1 us: intensity_of(): frames.reshape(layers_here, angles_here, rows_here, blocks, columns // bl...]
  transfers between devices with their start and end apart: 7 -> 8, of which waited for: 5 -> 1; matrix products, arithmetic and copies ran while one was open for 2% -> 2% of each run, Pallas kernels for 0% -> 26%
where the time goes in v1:
time: 40.5 us; the launch traced here: 40.1 us
  Pallas kernels  17.8 us (44%)
  starting transfers between devices  15.5 us (38%)
  waiting for transfers between devices  3.29 us (8%)
  local copies, waits for them, and re-layouts  2.65 us (7%)
  between operations  0.78 us (2%)
    pallas_call x2, Pallas kernels, partial_moments(): pl.pallas_call(functools.partial(moments_body, shift, count, steps), out_...  12.9 us
    ppermute x2, starting transfers between devices, both_sides(): lax.ppermute(tail, axis, [(i, i + 1) for i in range(count - 1)])  5.61 us
    ppermute x1, starting transfers between devices, on_device(): odd = lax.ppermute(odd, 'tile', swap_pairs(tiles, 1))  3.53 us
    ppermute x2, waiting for transfers between devices, both_sides(): lax.ppermute(head, axis, [(i + 1, i) for i in range(count - 1)])  3.27 us
    ppermute x2, starting transfers between devices, both_sides(): lax.ppermute(head, axis, [(i + 1, i) for i in range(count - 1)])  2.57 us
    ppermute x1, starting transfers between devices, on_device(): lax.ppermute(low, 'angle', pairs)  2.12 us
    unnamed x16, local copies, waits for them, and re-layouts  1.82 us
    pallas_call x1, Pallas kernels, spread_of(): pl.pallas_call(functools.partial(spread_body, len(parts) + 1), out_shape=...  1.7 us
  transfers between devices with their start and end apart: 8, of which 1 were waited for; matrix products, arithmetic and copies ran while one was open for 2% of the time, Pallas kernels for 26%

profile of v1, /device:TPU:1, one launch (start us, length us, event | category | flops | bytes accessed | tf_op | source)
XLA Modules:
  0.0 40.1 jit_solution(11127178539551793041)
XLA Ops:
  0.6 5.8 %moments_1.1 = (f32[3,24,256]{2,1,0:T(8,128)}, f32[3,24,256]{2,1,0:T(8,128)}) custom-call(s32[24,4,512]{2,1,0:T(4,128)} %bitcast.6, bf16[512,24,512]{2,1,0:T(8,128)(2,1)} %bitcast.4), custom_call_target="tpu_custom_call" | custom-call | flops 1610612736 | bytes 6291456 | tf_op jit(solution)/shard_map/moments_1/pallas_call | solution.py:91
  6.4 2.1 %collective-permute-start = (f32[3,24,256]{2,1,0:T(8,128)}, f32[3,24,256]{2,1,0:T(8,128)S(1)}, u32[]{:S(2)}, u32[]{:S(2)}) collective-permute-start(f32[3,24,256]{2,1,0:T(8,128)} %get-tuple-element.13), channel_id=1, source_target_pairs={{0,16},{16,0},{1,17},{17,1},{2,18},{18,2},{3,19},{19,3},{4,20},{20... | collective-permute-start | bytes 221192 | tf_op jit(solution)/shard_map/ppermute | solution.py:232
  8.5 0.1 collective-permute-start.1
  8.6 7.1 %moments_0.1 = (f32[3,24,256]{2,1,0:T(8,128)}, f32[3,24,256]{2,1,0:T(8,128)}) custom-call(s32[24,4,512]{2,1,0:T(4,128)} %bitcast.7, bf16[512,24,512]{2,1,0:T(8,128)(2,1)} %bitcast.5), custom_call_target="tpu_custom_call" | custom-call | flops 1610612736 | bytes 6291456 | tf_op jit(solution)/shard_map/moments_0/pallas_call | solution.py:91
  15.8 0.0 collective-permute-done.refs_0_
  15.8 0.0 copy-start
  15.8 0.6 %copy-done = f32[3,24,256]{2,1,0:T(8,128)} copy-done((f32[3,24,256]{2,1,0:T(8,128)}, f32[3,24,256]{2,1,0:T(8,128)S(1)}, u32[]{:S(2)}) %copy-start) | copy-done | bytes 73752
  16.4 1.6 %field.1 = (f32[2,24,256]{2,1,0:T(8,128)}, f32[2,1,256]{2,1,0:T(1,128)}, f32[2,1,256]{2,1,0:T(1,128)}) custom-call(f32[3,24,256]{2,1,0:T(8,128)} %get-tuple-element.12.own_ref.low_ref, f32[3,24,256]{2,1,0:T(8,128)} %copy-done), custom_call_target="tpu_custom_call" | custom-call | tf_op jit(solution)/shard_map/field/pallas_call | solution.py:131
  17.9 1.3 %collective-permute-start.7 = (f32[2,24,256]{2,1,0:T(8,128)}, f32[2,24,256]{2,1,0:T(8,128)S(1)}, u32[]{:S(2)}, u32[]{:S(2)}) collective-permute-start(f32[2,24,256]{2,1,0:T(8,128)} %get-tuple-element.14.field_ref), channel_id=1, source_target_pairs={{1,0},{3,2},{5,4},{7,6},{9,8},{11,10},{13,12},{15,14},{17,16},{19,... | collective-permute-start | bytes 147464 | tf_op jit(solution)/shard_map/ppermute | solution.py:220
  19.2 4.0 %collective-permute-start.6 = (f32[2,24,256]{2,1,0:T(8,128)}, f32[2,24,256]{2,1,0:T(8,128)S(1)}, u32[]{:S(2)}, u32[]{:S(2)}) collective-permute-start(f32[2,24,256]{2,1,0:T(8,128)} %get-tuple-element.14.field_ref), channel_id=1, source_target_pairs={{0,1},{2,3},{4,5},{6,7},{8,9},{10,11},{12,13},{14,15},{16,17},{18,... | collective-permute-start | bytes 147464 | tf_op jit(solution)/shard_map/ppermute | solution.py:219
  23.2 1.6 %collective-permute-start.2 = (f32[2,1,256]{2,1,0:T(1,128)}, f32[2,1,256]{2,1,0:T(1,128)S(1)}, u32[]{:S(2)}, u32[]{:S(2)}) collective-permute-start(f32[2,1,256]{2,1,0:T(1,128)} %get-tuple-element.19), channel_id=1, source_target_pairs={{0,2},{2,0},{4,6},{6,4},{8,10},{10,8},{12,14},{14,12},{1,3},{3,1},... | collective-permute-start | bytes 6152 | tf_op jit(solution)/shard_map/ppermute | solution.py:237
  24.8 3.5 %collective-permute-start.3 = (f32[2,1,256]{2,1,0:T(1,128)}, f32[2,1,256]{2,1,0:T(1,128)S(1)}, u32[]{:S(2)}, u32[]{:S(2)}) collective-permute-start(f32[2,1,256]{2,1,0:T(1,128)} %get-tuple-element.20), channel_id=1, source_target_pairs={{2,4},{4,2},{6,8},{8,6},{10,12},{12,10},{3,5},{5,3},{7,9},{9,7},{1... | collective-permute-start | bytes 6152 | tf_op jit(solution)/shard_map/ppermute | solution.py:238
  28.3 0.8 %fusion = (f32[2,24,1]{2,1,0:T(8,128)S(1)}, f32[2,24,1]{2,1,0:T(8,128)S(1)}) fusion(f32[2,24,256]{2,1,0:T(8,128)} %get-tuple-element.14.field_ref), kind=kLoop, calls=%fused_computation | loop fusion | bytes 768 | tf_op jit(solution)/shard_map/slice | solution.py:239
  29.2 0.0 collective-permute-done.1.refs_1_
  29.2 0.0 copy-start.1
  29.2 1.3 %collective-permute-start.5 = (f32[2,24,1]{2,1,0:T(8,128)S(1)}, f32[2,24,1]{2,1,0:T(8,128)S(1)}, u32[]{:S(2)}, u32[]{:S(2)}) collective-permute-start(f32[2,24,1]{2,1,0:T(8,128)S(1)} %get-tuple-element.21), channel_id=1, source_target_pairs={{16,0},{17,1},{18,2},{19,3},{20,4},{21,5},{22,6},{23,7},{24,8},{25... | collective-permute-start | bytes 584 | tf_op jit(solution)/shard_map/ppermute | solution.py:220
  30.5 3.3 %collective-permute-done.5.right_ref = f32[2,24,1]{2,1,0:T(8,128)S(1)} collective-permute-done((f32[2,24,1]{2,1,0:T(8,128)S(1)}, f32[2,24,1]{2,1,0:T(8,128)S(1)}, u32[]{:S(2)}, u32[]{:S(2)}) %collective-permute-start.5) | collective-permute-done | bytes 224 | tf_op jit(solution)/shard_map/ppermute | solution.py:220
  33.7 0.0 copy-start.4
  33.8 1.6 %collective-permute-start.4 = (f32[2,24,1]{2,1,0:T(8,128)S(1)}, f32[2,24,1]{2,1,0:T(8,128)S(1)}, u32[]{:S(2)}, u32[]{:S(2)}) collective-permute-start(f32[2,24,1]{2,1,0:T(8,128)S(1)} %get-tuple-element.22), channel_id=1, source_target_pairs={{0,16},{1,17},{2,18},{3,19},{4,20},{5,21},{6,22},{7,23},{8,24},{9,... | collective-permute-start | bytes 584 | tf_op jit(solution)/shard_map/ppermute | solution.py:219
  35.4 0.0 copy-done.1
  35.4 1.7 %spread.1 = (f32[2,1,24,256]{3,2,1,0:T(8,128)}, f32[3,1,24,256]{3,2,1,0:T(8,128)}) custom-call(s32[1,24,256]{2,1,0:T(8,128)} %mask_ref.3, f32[2,24,256]{2,1,0:T(8,128)} %get-tuple-element.14.field_ref, f32[3,24,256]{2,1,0:T(8,128)} %get-tuple-element.12.own_ref.low_ref, f32[3,24,256]{2,1,0:T(8,128)} %get-tuple-element.15.high_ref, f32[3,24,256]{2,1,0:T(8,128)} %copy-done, ...), custom_call_target="tpu_custom_call" | custom-call | tf_op jit(solution)/shard_map/spread/pallas_call | solution.py:159
  37.1 0.0 collective-permute-done.4.left_ref
  37.1 0.0 copy-start.5
  37.1 0.0 collective-permute-done.2.even_ref
  37.1 0.0 copy-start.6
  37.1 0.0 collective-permute-done.3.odd_ref
  37.1 0.0 copy-start.7
  37.1 0.0 collective-permute-done.7.above_ref
  37.1 0.0 copy-start.2
  37.2 0.0 collective-permute-done.6.below_ref
  37.2 0.0 copy-done.4
  37.2 0.5 %copy-done.5 = f32[2,24,1]{2,1,0:T(8,128)} copy-done((f32[2,24,1]{2,1,0:T(8,128)}, f32[2,24,1]{2,1,0:T(8,128)S(1)}, u32[]{:S(2)}) %copy-start.5) | copy-done | bytes 216
  37.7 0.0 copy-done.6
  37.7 0.0 copy-done.7
  37.7 0.0 copy-done.2
  37.8 0.0 copy-start.3
  37.8 0.6 %copy-done.3 = f32[2,24,256]{2,1,0:T(8,128)} copy-done((f32[2,24,256]{2,1,0:T(8,128)}, f32[2,24,256]{2,1,0:T(8,128)S(1)}, u32[]{:S(2)}) %copy-start.3) | copy-done | bytes 49176
  38.4 1.7 %nye.1 = f32[7,1,24,256]{3,2,1,0:T(8,128)} custom-call(s32[1,24,256]{2,1,0:T(8,128)} %mask_ref.3, f32[2,24,256]{2,1,0:T(8,128)} %get-tuple-element.14.field_ref, f32[2,1,256]{2,1,0:T(1,128)} %copy-done.6, f32[2,1,256]{2,1,0:T(1,128)} %copy-done.7, f32[2,24,1]{2,1,0:T(8,128)} %copy-done.5, f32[2,24,1]{2,1,0:T(8,128)} %copy-done.4, f32[2,24,256]{2,1,0:T(8,128)} %copy-done.3, ...), custom_call_target="tpu_custom_call" | custom-call | tf_op jit(solution)/shard_map/nye/pallas_call | solution.py:200
Async XLA Ops:
  6.4 9.4 %collective-permute-start = (f32[3,24,256]{2,1,0:T(8,128)}, f32[3,24,256]{2,1,0:T(8,128)S(1)}, u32[]{:S(2)}, u32[]{:S(2)}) collective-permute-start(f32[3,24,256]{2,1,0:T(8,128)} %get-tuple-element.13), channel_id=1, source_target_pairs={{0,16},{16,0},{1,17},{17,1},{2,18},{18,2},{3,19},{19,3},{4,20},{20... | collective-permute-start | bytes 221192 | tf_op jit(solution)/shard_map/ppermute | solution.py:232
  8.5 20.6 %collective-permute-start.1 = (f32[3,24,256]{2,1,0:T(8,128)}, f32[3,24,256]{2,1,0:T(8,128)S(1)}, u32[]{:S(2)}, u32[]{:S(2)}) collective-permute-start(f32[3,24,256]{2,1,0:T(8,128)} %get-tuple-element.16), channel_id=1, source_target_pairs={{0,16},{16,0},{1,17},{17,1},{2,18},{18,2},{3,19},{19,3},{4,20},{20... | collective-permute-start | bytes 221192 | tf_op jit(solution)/shard_map/ppermute | solution.py:232
  15.8 0.6 %copy-start = (f32[3,24,256]{2,1,0:T(8,128)}, f32[3,24,256]{2,1,0:T(8,128)S(1)}, u32[]{:S(2)}) copy-start(f32[3,24,256]{2,1,0:T(8,128)S(1)} %collective-permute-done.refs_0_) | copy-start | bytes 221188
  17.9 19.2 %collective-permute-start.7 = (f32[2,24,256]{2,1,0:T(8,128)}, f32[2,24,256]{2,1,0:T(8,128)S(1)}, u32[]{:S(2)}, u32[]{:S(2)}) collective-permute-start(f32[2,24,256]{2,1,0:T(8,128)} %get-tuple-element.14.field_ref), channel_id=1, source_target_pairs={{1,0},{3,2},{5,4},{7,6},{9,8},{11,10},{13,12},{15,14},{17,16},{19,... | collective-permute-start | bytes 147464 | tf_op jit(solution)/shard_map/ppermute | solution.py:220
  19.2 17.9 %collective-permute-start.6 = (f32[2,24,256]{2,1,0:T(8,128)}, f32[2,24,256]{2,1,0:T(8,128)S(1)}, u32[]{:S(2)}, u32[]{:S(2)}) collective-permute-start(f32[2,24,256]{2,1,0:T(8,128)} %get-tuple-element.14.field_ref), channel_id=1, source_target_pairs={{0,1},{2,3},{4,5},{6,7},{8,9},{10,11},{12,13},{14,15},{16,17},{18,... | collective-permute-start | bytes 147464 | tf_op jit(solution)/shard_map/ppermute | solution.py:219
  23.2 13.9 %collective-permute-start.2 = (f32[2,1,256]{2,1,0:T(1,128)}, f32[2,1,256]{2,1,0:T(1,128)S(1)}, u32[]{:S(2)}, u32[]{:S(2)}) collective-permute-start(f32[2,1,256]{2,1,0:T(1,128)} %get-tuple-element.19), channel_id=1, source_target_pairs={{0,2},{2,0},{4,6},{6,4},{8,10},{10,8},{12,14},{14,12},{1,3},{3,1},... | collective-permute-start | bytes 6152 | tf_op jit(solution)/shard_map/ppermute | solution.py:237
  24.8 12.3 %collective-permute-start.3 = (f32[2,1,256]{2,1,0:T(1,128)}, f32[2,1,256]{2,1,0:T(1,128)S(1)}, u32[]{:S(2)}, u32[]{:S(2)}) collective-permute-start(f32[2,1,256]{2,1,0:T(1,128)} %get-tuple-element.20), channel_id=1, source_target_pairs={{2,4},{4,2},{6,8},{8,6},{10,12},{12,10},{3,5},{5,3},{7,9},{9,7},{1... | collective-permute-start | bytes 6152 | tf_op jit(solution)/shard_map/ppermute | solution.py:238
  29.2 6.2 %copy-start.1 = (f32[3,24,256]{2,1,0:T(8,128)}, f32[3,24,256]{2,1,0:T(8,128)S(1)}, u32[]{:S(2)}) copy-start(f32[3,24,256]{2,1,0:T(8,128)S(1)} %collective-permute-done.1.refs_1_) | copy-start | bytes 221188
  29.2 4.6 %collective-permute-start.5 = (f32[2,24,1]{2,1,0:T(8,128)S(1)}, f32[2,24,1]{2,1,0:T(8,128)S(1)}, u32[]{:S(2)}, u32[]{:S(2)}) collective-permute-start(f32[2,24,1]{2,1,0:T(8,128)S(1)} %get-tuple-element.21), channel_id=1, source_target_pairs={{16,0},{17,1},{18,2},{19,3},{20,4},{21,5},{22,6},{23,7},{24,8},{25... | collective-permute-start | bytes 584 | tf_op jit(solution)/shard_map/ppermute | solution.py:220
  33.7 3.4 %copy-start.4 = (f32[2,24,1]{2,1,0:T(8,128)}, f32[2,24,1]{2,1,0:T(8,128)S(1)}, u32[]{:S(2)}) copy-start(f32[2,24,1]{2,1,0:T(8,128)S(1)} %collective-permute-done.5.right_ref) | copy-start | bytes 580
  33.8 3.3 %collective-permute-start.4 = (f32[2,24,1]{2,1,0:T(8,128)S(1)}, f32[2,24,1]{2,1,0:T(8,128)S(1)}, u32[]{:S(2)}, u32[]{:S(2)}) collective-permute-start(f32[2,24,1]{2,1,0:T(8,128)S(1)} %get-tuple-element.22), channel_id=1, source_target_pairs={{0,16},{1,17},{2,18},{3,19},{4,20},{5,21},{6,22},{7,23},{8,24},{9,... | collective-permute-start | bytes 584 | tf_op jit(solution)/shard_map/ppermute | solution.py:219
  37.1 0.6 %copy-start.5 = (f32[2,24,1]{2,1,0:T(8,128)}, f32[2,24,1]{2,1,0:T(8,128)S(1)}, u32[]{:S(2)}) copy-start(f32[2,24,1]{2,1,0:T(8,128)S(1)} %collective-permute-done.4.left_ref) | copy-start | bytes 580
  37.1 0.6 %copy-start.6 = (f32[2,1,256]{2,1,0:T(1,128)}, f32[2,1,256]{2,1,0:T(1,128)S(1)}, u32[]{:S(2)}) copy-start(f32[2,1,256]{2,1,0:T(1,128)S(1)} %collective-permute-done.2.even_ref) | copy-start | bytes 6148
  37.1 0.6 %copy-start.7 = (f32[2,1,256]{2,1,0:T(1,128)}, f32[2,1,256]{2,1,0:T(1,128)S(1)}, u32[]{:S(2)}) copy-start(f32[2,1,256]{2,1,0:T(1,128)S(1)} %collective-permute-done.3.odd_ref) | copy-start | bytes 6148
  37.1 0.6 %copy-start.2 = (f32[2,24,256]{2,1,0:T(8,128)}, f32[2,24,256]{2,1,0:T(8,128)S(1)}, u32[]{:S(2)}) copy-start(f32[2,24,256]{2,1,0:T(8,128)S(1)} %collective-permute-done.7.above_ref) | copy-start | bytes 147460
  37.8 0.6 %copy-start.3 = (f32[2,24,256]{2,1,0:T(8,128)}, f32[2,24,256]{2,1,0:T(8,128)S(1)}, u32[]{:S(2)}) copy-start(f32[2,24,256]{2,1,0:T(8,128)S(1)} %collective-permute-done.6.below_ref) | copy-start | bytes 147460

commit v2 on v1

--- a/solution.py
+++ b/solution.py
@@ -12,10 +12,13 @@
 F32 = jnp.float32
 BF16 = jnp.bfloat16
 VMEM = pl.BlockSpec(memory_space=pltpu.VMEM)
-ANY = pl.BlockSpec(memory_space=pl.ANY)
-
-
-def moments_body(shift, count, steps, e_hbm, f_hbm, low_ref, high_ref, buf, ebuf, sem, esem):
+ANY = pl.BlockSpec(memory_space=pltpu.HBM)
+
+
+STEPS = 4
+
+
+def moments_body(shift, count, steps, e_hbm, f_hbm, low_ref, high_ref, buf, ebuf, fbuf, sem, esem):
     angles, rows, width = buf.shape
     blocks = ebuf.shape[1]
     span = f_hbm.shape[2] // blocks
@@ -35,59 +38,72 @@
         )
         copy.start()
         copies.append(copy)
-    low_ref[...] = jnp.zeros_like(low_ref)
-    high_ref[...] = jnp.zeros_like(high_ref)
     lane = lax.broadcasted_iota(jnp.int32, (8, deep), 1)
     diagonal = (lane & 7) == lax.broadcasted_iota(jnp.int32, (8, deep), 0)
     chi = ((lane >> 3).astype(F32) - 0.5 * (NCHI - 1)) / (0.5 * NCHI)
-    chi_chi = (chi * chi).astype(BF16).astype(F32)
+    chi_chi = chi * chi
     source = lax.broadcasted_iota(jnp.int32, (128, deep), 0)
     target = lax.broadcasted_iota(jnp.int32, (128, deep), 1) >> 3
-    spread_out = [
-        (source == target + NCHI * part).astype(F32).astype(BF16) for part in range(128 // NCHI)
-    ]
+    per = 128 // NCHI
     exponent_copy.wait()
+    pieces = angles // 128
+    picked = lax.broadcasted_iota(jnp.int32, (here * rows, rows * blocks), 0)
+    natural = lax.broadcasted_iota(jnp.int32, (here * rows, rows * blocks), 1)
+    picked = sum(
+        (natural == (picked - b * rows) * blocks + block * here + b) & (picked >= b * rows) & (picked < (b + 1) * rows)
+        for b in range(here)
+    )
+    factor = jnp.exp2(ebuf[...].reshape(rows * blocks, angles).astype(F32)).astype(BF16)
+    factor = jnp.dot(picked.astype(F32).astype(BF16), factor, preferred_element_type=F32)
     factor = jnp.concatenate(
-        [
-            jnp.exp2(ebuf[:, pl.ds(block * here + b, 1), :].reshape(rows, angles).astype(F32))
-            for b in range(here)
-        ],
-        0,
+        [factor[:, c * 128 : (c + 1) * 128] for c in range(pieces)], 0
     ).astype(BF16)
+    for part in range(per):
+        one_hot = (source == target + NCHI * part).astype(F32).astype(BF16)
+        fbuf[part] = jnp.dot(factor, one_hot, preferred_element_type=F32)
     first_phi = me * (angles // NCHI)
-    for g in range(angles // NCHI):
-        if (g * NCHI) % size == 0:
-            copies[(g * NCHI) // size].wait()
-        chunk = g * NCHI // 128 * 128
-        factors = jnp.dot(
-            factor[:, chunk : chunk + 128],
-            spread_out[g % (128 // NCHI)],
-            preferred_element_type=F32,
-        )
-        phi = ((first_phi + g).astype(F32) - 0.5 * (NPHI - 1)) / (0.5 * NPHI)
-        phi_chi = (phi * chi).astype(BF16).astype(F32)
-        phi_phi = jnp.full((8, 128), phi * phi, F32).astype(BF16).astype(F32)[:, :1]
+    groups = size // NCHI
+    for step in range(steps):
+        copies[step].wait()
         for r in range(rows // 8):
             at_rows = slice(r * 8, r * 8 + 8)
             for b in range(here):
                 at_columns = slice(b * span, (b + 1) * span)
-                top = b * rows + r * 8
-                unit = jnp.where(diagonal, factors[top : top + 8], 0.0)
-                left = jnp.concatenate([unit, unit * chi, unit * chi_chi, unit * phi_chi], 0)
-                cells = buf[g * NCHI : (g + 1) * NCHI, at_rows, at_columns].reshape(deep, span)
-                sums = jnp.dot(left.astype(BF16), cells, preferred_element_type=F32)
-                low_ref[0, at_rows, at_columns] += sums[:8]
-                low_ref[1, at_rows, at_columns] += sums[:8] * phi
-                low_ref[2, at_rows, at_columns] += sums[8:16]
-                high_ref[0, at_rows, at_columns] += sums[:8] * phi_phi
-                high_ref[1, at_rows, at_columns] += sums[16:24]
-                high_ref[2, at_rows, at_columns] += sums[24:]
+                left = []
+                for g in range(step * groups, (step + 1) * groups):
+                    phi = ((first_phi + g).astype(F32) - 0.5 * (NPHI - 1)) / (0.5 * NPHI)
+                    top = ((g // per) * here + b) * rows + r * 8
+                    unit = jnp.where(diagonal, fbuf[g % per, top : top + 8], 0.0)
+                    left.append(
+                        jnp.concatenate(
+                            [
+                                unit,
+                                unit * phi,
+                                unit * chi,
+                                unit * (phi * phi),
+                                unit * chi_chi,
+                                unit * (phi * chi),
+                            ],
+                            0,
+                        ).astype(BF16)
+                    )
+                left = jnp.concatenate(left, 1)
+                cells = buf[step * size : (step + 1) * size, at_rows, at_columns].reshape(size * 8, span)
+                sums = jnp.dot(left, cells, preferred_element_type=F32)
+                for m in range(6):
+                    ref, k = (low_ref, m) if m < 3 else (high_ref, m - 3)
+                    value = sums[m * 8 : m * 8 + 8]
+                    if step:
+                        value = value + ref[k, at_rows, at_columns]
+                    ref[k, at_rows, at_columns] = value
 
 
 def partial_moments(frames, exponents, shift, count):
     angles, rows, columns = frames.shape
     width = columns // count
-    steps = 8
+    steps = STEPS
+    here = width * exponents.shape[1] // columns
+    scratch = (angles // 128 * here * rows, NCHI * 8)
     return pl.pallas_call(
         functools.partial(moments_body, shift, count, steps),
         out_shape=[jax.ShapeDtypeStruct((3, rows, width), F32)] * 2,
@@ -96,10 +112,12 @@
         scratch_shapes=[
             pltpu.VMEM((angles, rows, width), BF16),
             pltpu.VMEM(exponents.shape, jnp.int32),
+            pltpu.VMEM((128 // NCHI, *scratch), F32),
             pltpu.SemaphoreType.DMA((steps,)),
             pltpu.SemaphoreType.DMA,
         ],
         name=f"moments_{shift}",
+        compiler_params=pltpu.CompilerParams(vmem_limit_bytes=24 << 20),
         cost_estimate=pl.CostEstimate(
             flops=512 * angles * rows * width,
             bytes_accessed=2 * angles * rows * width,
@@ -134,6 +152,7 @@
         in_specs=[VMEM] * (len(parts) + 1),
         out_specs=[VMEM] * 3,
         name="field",
+        compiler_params=pltpu.CompilerParams(vmem_limit_bytes=4 << 20),
     )(own, *parts)
 
 
@@ -165,10 +184,11 @@
         in_specs=[VMEM] * (4 + len(flat)),
         out_specs=[VMEM] * 2,
         name="spread",
+        compiler_params=pltpu.CompilerParams(vmem_limit_bytes=4 << 20),
     )(mask, field, low, high, *flat)
 
 
-def nye_body(mask_ref, field_ref, even_ref, odd_ref, left_ref, right_ref, below_ref, above_ref, nye_ref):
+def nye_body(pair, mask_ref, field_ref, even_ref, odd_ref, left_ref, right_ref, below_ref, above_ref, nye_ref):
     rows, width = field_ref.shape[1:]
     mask = mask_ref[0].astype(F32)
     is_even = lax.rem(lax.axis_index("tile"), 2) == 0
@@ -185,7 +205,12 @@
         before = jnp.where(column == 0, left_ref[c], pltpu.roll(value, 1, 1))
         after = jnp.where(column == width - 1, right_ref[c], pltpu.roll(value, width - 1, 1))
         along_x.append(0.5 * (after - before))
-        along_z.append((0.5 / layer_pitch) * (above_ref[c] - below_ref[c]))
+        lower_layer, upper_layer = below_ref[c], above_ref[c]
+        if pair:
+            is_first = lax.axis_index("layer") == 0
+            lower_layer = jnp.where(is_first, 0.0, lower_layer)
+            upper_layer = jnp.where(is_first, upper_layer, 0.0)
+        along_z.append((0.5 / layer_pitch) * (upper_layer - lower_layer))
     nye_ref[0, 0] = -along_y[1] * mask
     nye_ref[1, 0] = -along_x[0] * mask
     nye_ref[2, 0] = -(along_x[0] + along_y[1]) * mask
@@ -195,14 +220,15 @@
     nye_ref[6, 0] = along_z[1] * mask
 
 
-def nye_of(mask, field, even, odd, left, right, below, above):
+def nye_of(pair, mask, field, even, odd, left, right, below, above):
     _, rows, width = field.shape
     return pl.pallas_call(
-        nye_body,
+        functools.partial(nye_body, pair),
         out_shape=jax.ShapeDtypeStruct((7, 1, rows, width), F32),
         in_specs=[VMEM] * 8,
         out_specs=VMEM,
         name="nye",
+        compiler_params=pltpu.CompilerParams(vmem_limit_bytes=4 << 20),
     )(mask, field, even, odd, left, right, below, above)
 
 
@@ -215,6 +241,10 @@
 
 def both_sides(tail, head, axis):
     count = lax.axis_size(axis)
+    if count == 2:
+        first = lax.axis_index(axis) == 0
+        other = lax.ppermute(jnp.where(first, tail, head), axis, [(0, 1), (1, 0)])
+        return jnp.where(first, 0.0, other), jnp.where(first, other, 0.0)
     return (
         lax.ppermute(tail, axis, [(i, i + 1) for i in range(count - 1)]),
         lax.ppermute(head, axis, [(i + 1, i) for i in range(count - 1)]),
@@ -223,8 +253,8 @@
 
 def on_device(frames, exponents, valid_mask):
     count = lax.axis_size("angle")
-    frames = frames[0]
-    exponents = exponents[0].transpose(1, 2, 0)
+    frames = pltpu.with_memory_space_constraint(frames[0], pltpu.HBM)
+    exponents = pltpu.with_memory_space_constraint(exponents[0].transpose(1, 2, 0), pltpu.HBM)
     sent = []
     for shift in range(1, count):
         low, high = partial_moments(frames, exponents, shift, count)
@@ -232,13 +262,17 @@
         sent.append((lax.ppermute(low, "angle", pairs), lax.ppermute(high, "angle", pairs)))
     low, high = partial_moments(frames, exponents, 0, count)
     field, even, odd = field_of(low, [part[0] for part in sent])
-    below, above = both_sides(field, field, "layer")
+    if lax.axis_size("layer") == 2:
+        other = lax.ppermute(field, "layer", [(0, 1), (1, 0)])
+        below, above = other, other
+    else:
+        below, above = both_sides(field, field, "layer")
     tiles = lax.axis_size("tile")
     even = lax.ppermute(even, "tile", swap_pairs(tiles, 0))
     odd = lax.ppermute(odd, "tile", swap_pairs(tiles, 1))
     left, right = both_sides(field[:, :, -1:], field[:, :, :1], "angle")
     orient, spread = spread_of(valid_mask, field, low, high, sent)
-    nye = nye_of(valid_mask, field, even, odd, left, right, below, above)
+    nye = nye_of(lax.axis_size("layer") == 2, valid_mask, field, even, odd, left, right, below, above)
     return orient, spread, nye
 
 

time: 40.5 us -> 19.2 us (0.47)
  Pallas kernels: 17.8 us -> 8.17 us
  starting transfers between devices: 15.5 us -> 9.28 us
  local copies, waits for them, and re-layouts: 2.65 us -> 0.01 us
  waiting for transfers between devices: 3.29 us -> 0.77 us
    pallas_call x2, Pallas kernels: 12.9 us -> 6.7 us  [partial_moments(): pl.pallas_call(functools.partial(moments_body, shift, count, steps), out_...]
    ppermute x4 -> x2, starting transfers between devices: 8.18 us -> 2.52 us  [the longest x1 1.28 us: on_device(): other = lax.ppermute(field, 'layer', [(0, 1), (1, 0)])]
    ppermute x4 -> x2, waiting for transfers between devices: 3.28 us -> 0.76 us  [the longest x1 0.76 us: both_sides(): other = lax.ppermute(jnp.where(first, tail, head), axis, [(0, 1), (1, 0)])]
    unnamed x16 -> x2, local copies, waits for them, and re-layouts: 1.82 us -> 0.01 us
    pallas_call x1, Pallas kernels: 1.55 us -> 0.02 us  [field_of(): pl.pallas_call(functools.partial(field_body, len(parts) + 1), out_shape=[...]
    pallas_call x1, Pallas kernels: 1.7 us -> 0.67 us  [spread_of(): pl.pallas_call(functools.partial(spread_body, len(parts) + 1), out_shape=...]
    pallas_call x1, Pallas kernels: 1.68 us -> 0.78 us  [nye_of(): pl.pallas_call(functools.partial(nye_body, pair), out_shape=jax.ShapeDtyp...]
    slice x1 -> x0, local copies, waits for them, and re-layouts: 0.83 us -> none  [on_device(): left, right = both_sides(field[:, :, -1:], field[:, :, :1], 'angle')]
  transfers between devices with their start and end apart: 8 -> 6, of which waited for: 1 -> 1; matrix products, arithmetic and copies ran while one was open for 2% -> 0% of each run, Pallas kernels for 26% -> 21%
where the time goes in v2:
time: 19.2 us; the launch traced here: 19 us
  starting transfers between devices  9.28 us (48%)
  Pallas kernels  8.17 us (43%)
  waiting for transfers between devices  0.77 us (4%)
  between operations  0.71 us (4%)
    pallas_call x2, Pallas kernels, partial_moments(): pl.pallas_call(functools.partial(moments_body, shift, count, steps), out_...  6.7 us
    ppermute x1, starting transfers between devices, on_device(): odd = lax.ppermute(odd, 'tile', swap_pairs(tiles, 1))  3.53 us
    ppermute x1, starting transfers between devices, on_device(): lax.ppermute(low, 'angle', pairs)  2.12 us
    ppermute x1, starting transfers between devices, on_device(): other = lax.ppermute(field, 'layer', [(0, 1), (1, 0)])  1.28 us
    ppermute x1, starting transfers between devices, both_sides(): other = lax.ppermute(jnp.where(first, tail, head), axis, [(0, 1), (1, 0)])  1.25 us
    ppermute x1, starting transfers between devices, on_device(): even = lax.ppermute(even, 'tile', swap_pairs(tiles, 0))  1.02 us
    pallas_call x1, Pallas kernels, nye_of(): pl.pallas_call(functools.partial(nye_body, pair), out_shape=jax.ShapeDtyp...  0.78 us
    ppermute x1, waiting for transfers between devices, both_sides(): other = lax.ppermute(jnp.where(first, tail, head), axis, [(0, 1), (1, 0)])  0.76 us
  transfers between devices with their start and end apart: 6, of which 1 were waited for; matrix products, arithmetic and copies ran while one was open for 0% of the time, Pallas kernels for 21%

profile of v2, /device:TPU:1, one launch (start us, length us, event | category | flops | bytes accessed | tf_op | source)
XLA Modules:
  0.0 19.0 jit_solution(11004545424794850151)
XLA Ops:
  0.6 0.0 copy-start
  0.6 3.3 %moments_1.1 = (f32[3,24,256]{2,1,0:T(8,128)S(1)}, f32[3,24,256]{2,1,0:T(8,128)S(1)}) custom-call(s32[24,4,512]{2,1,0:T(4,128)} %bitcast.6, bf16[512,24,512]{2,1,0:T(8,128)(2,1)} %bitcast.4), custom_call_target="tpu_custom_call" | custom-call | flops 1610612736 | bytes 6291456 | tf_op jit(solution)/shard_map/moments_1/pallas_call | solution.py:107
  4.0 2.1 %collective-permute-start = (f32[3,24,256]{2,1,0:T(8,128)S(1)}, f32[3,24,256]{2,1,0:T(8,128)S(1)}, u32[]{:S(2)}, u32[]{:S(2)}) collective-permute-start(f32[3,24,256]{2,1,0:T(8,128)S(1)} %get-tuple-element.13), channel_id=1, source_target_pairs={{0,16},{16,0},{1,17},{17,1},{2,18},{18,2},{3,19},{19,3},{4,20},{20... | collective-permute-start | bytes 221192 | tf_op jit(solution)/shard_map/ppermute | solution.py:262
  6.1 0.1 collective-permute-start.1
  6.2 3.3 %moments_0.1 = (f32[3,24,256]{2,1,0:T(8,128)S(1)}, f32[3,24,256]{2,1,0:T(8,128)S(1)}) custom-call(s32[24,4,512]{2,1,0:T(4,128)} %bitcast.7, bf16[512,24,512]{2,1,0:T(8,128)(2,1)} %bitcast.5), custom_call_target="tpu_custom_call" | custom-call | flops 1610612736 | bytes 6291456 | tf_op jit(solution)/shard_map/moments_0/pallas_call | solution.py:107
  9.6 0.0 collective-permute-done.refs_0_
  9.6 1.0 %collective-permute-start.2 = (f32[2,1,256]{2,1,0:T(1,128)S(1)}, f32[2,1,256]{2,1,0:T(1,128)S(1)}, u32[]{:S(2)}, u32[]{:S(2)}) collective-permute-start(f32[2,1,256]{2,1,0:T(1,128)S(1)} %get-tuple-element.19), channel_id=1, source_target_pairs={{0,2},{2,0},{4,6},{6,4},{8,10},{10,8},{12,14},{14,12},{1,3},{3,1},... | collective-permute-start | bytes 6152 | tf_op jit(solution)/shard_map/ppermute | solution.py:271
  10.6 3.5 %collective-permute-start.3 = (f32[2,1,256]{2,1,0:T(1,128)S(1)}, f32[2,1,256]{2,1,0:T(1,128)S(1)}, u32[]{:S(2)}, u32[]{:S(2)}) collective-permute-start(f32[2,1,256]{2,1,0:T(1,128)S(1)} %get-tuple-element.20), channel_id=1, source_target_pairs={{2,4},{4,2},{6,8},{8,6},{10,12},{12,10},{3,5},{5,3},{7,9},{9,7},{1... | collective-permute-start | bytes 6152 | tf_op jit(solution)/shard_map/ppermute | solution.py:272
  14.2 1.3 %collective-permute-start.5 = (f32[2,24,256]{2,1,0:T(8,128)S(1)}, f32[2,24,256]{2,1,0:T(8,128)S(1)}, u32[]{:S(2)}, u32[]{:S(2)}) collective-permute-start(f32[2,24,256]{2,1,0:T(8,128)S(1)} %get-tuple-element.14.field_ref), channel_id=1, source_target_pairs={{0,1},{1,0},{2,3},{3,2},{4,5},{5,4},{6,7},{7,6},{8,9},{9,8},{10,11... | collective-permute-start | bytes 147464 | tf_op jit(solution)/shard_map/ppermute | solution.py:266
  15.4 0.1 slice_select_fusion
  15.5 1.2 %collective-permute-start.4 = (f32[2,24,1]{2,1,0:T(8,128)S(1)}, f32[2,24,1]{2,1,0:T(8,128)S(1)}, u32[]{:S(2)}, u32[]{:S(2)}) collective-permute-start(f32[2,24,1]{2,1,0:T(8,128)S(1)} %slice_select_fusion), channel_id=1, source_target_pairs={{0,16},{16,0},{1,17},{17,1},{2,18},{18,2},{3,19},{19,3},{4,20},{20... | collective-permute-start | bytes 584 | tf_op jit(solution)/shard_map/ppermute | solution.py:246
  16.8 0.0 collective-permute-done.1.refs_1_
  16.8 0.0 copy-done
  16.8 0.7 %spread.1 = (f32[2,1,24,256]{3,2,1,0:T(8,128)}, f32[3,1,24,256]{3,2,1,0:T(8,128)}) custom-call(s32[1,24,256]{2,1,0:T(8,128)S(1)} %copy-done, f32[2,24,256]{2,1,0:T(8,128)S(1)} %get-tuple-element.14.field_ref, f32[3,24,256]{2,1,0:T(8,128)S(1)} %get-tuple-element.12.own_ref.low_ref, f32[3,24,256]{2,1,0:T(8,128)S(1)} %get-tuple-element.15.high_ref, ...), custom_call_target="tpu_custom_call" | custom-call | tf_op jit(solution)/shard_map/spread/pallas_call | solution.py:178
  17.4 0.8 %collective-permute-done.4 = f32[2,24,1]{2,1,0:T(8,128)S(1)} collective-permute-done((f32[2,24,1]{2,1,0:T(8,128)S(1)}, f32[2,24,1]{2,1,0:T(8,128)S(1)}, u32[]{:S(2)}, u32[]{:S(2)}) %collective-permute-start.4) | collective-permute-done | bytes 224 | tf_op jit(solution)/shard_map/ppermute | solution.py:246
  18.2 0.0 collective-permute-done.2.even_ref
  18.2 0.0 collective-permute-done.3.odd_ref
  18.2 0.0 collective-permute-done.5.below_ref.above_ref
  18.2 0.8 %nye.1 = f32[7,1,24,256]{3,2,1,0:T(8,128)} custom-call(s32[1,24,256]{2,1,0:T(8,128)S(1)} %copy-done, f32[2,24,256]{2,1,0:T(8,128)S(1)} %get-tuple-element.14.field_ref, f32[2,1,256]{2,1,0:T(1,128)S(1)} %collective-permute-done.2.even_ref, f32[2,1,256]{2,1,0:T(1,128)S(1)} %collective-permute-done.3.odd_ref, f32[2,24,1]{2,1,0:T(8,128)S(1)} %get-tuple-element.22.left_ref, ...), custom_call_target="tpu_custom_call" | custom-call | tf_op jit(solution)/shard_map/nye/pallas_call | solution.py:225
  (2 shorter events, 0.0 us)
Async XLA Ops:
  0.6 16.1 %copy-start = (s32[1,24,256]{2,1,0:T(8,128)S(1)}, s32[1,24,256]{2,1,0:T(8,128)}, u32[]{:S(2)}) copy-start(s32[1,24,256]{2,1,0:T(8,128)} %mask_ref.3) | copy-start | bytes 73732
  4.0 5.6 %collective-permute-start = (f32[3,24,256]{2,1,0:T(8,128)S(1)}, f32[3,24,256]{2,1,0:T(8,128)S(1)}, u32[]{:S(2)}, u32[]{:S(2)}) collective-permute-start(f32[3,24,256]{2,1,0:T(8,128)S(1)} %get-tuple-element.13), channel_id=1, source_target_pairs={{0,16},{16,0},{1,17},{17,1},{2,18},{18,2},{3,19},{19,3},{4,20},{20... | collective-permute-start | bytes 221192 | tf_op jit(solution)/shard_map/ppermute | solution.py:262
  6.1 10.6 %collective-permute-start.1 = (f32[3,24,256]{2,1,0:T(8,128)S(1)}, f32[3,24,256]{2,1,0:T(8,128)S(1)}, u32[]{:S(2)}, u32[]{:S(2)}) collective-permute-start(f32[3,24,256]{2,1,0:T(8,128)S(1)} %get-tuple-element.16), channel_id=1, source_target_pairs={{0,16},{16,0},{1,17},{17,1},{2,18},{18,2},{3,19},{19,3},{4,20},{20... | collective-permute-start | bytes 221192 | tf_op jit(solution)/shard_map/ppermute | solution.py:262
  9.6 8.6 %collective-permute-start.2 = (f32[2,1,256]{2,1,0:T(1,128)S(1)}, f32[2,1,256]{2,1,0:T(1,128)S(1)}, u32[]{:S(2)}, u32[]{:S(2)}) collective-permute-start(f32[2,1,256]{2,1,0:T(1,128)S(1)} %get-tuple-element.19), channel_id=1, source_target_pairs={{0,2},{2,0},{4,6},{6,4},{8,10},{10,8},{12,14},{14,12},{1,3},{3,1},... | collective-permute-start | bytes 6152 | tf_op jit(solution)/shard_map/ppermute | solution.py:271
  10.6 7.6 %collective-permute-start.3 = (f32[2,1,256]{2,1,0:T(1,128)S(1)}, f32[2,1,256]{2,1,0:T(1,128)S(1)}, u32[]{:S(2)}, u32[]{:S(2)}) collective-permute-start(f32[2,1,256]{2,1,0:T(1,128)S(1)} %get-tuple-element.20), channel_id=1, source_target_pairs={{2,4},{4,2},{6,8},{8,6},{10,12},{12,10},{3,5},{5,3},{7,9},{9,7},{1... | collective-permute-start | bytes 6152 | tf_op jit(solution)/shard_map/ppermute | solution.py:272
  14.2 4.1 %collective-permute-start.5 = (f32[2,24,256]{2,1,0:T(8,128)S(1)}, f32[2,24,256]{2,1,0:T(8,128)S(1)}, u32[]{:S(2)}, u32[]{:S(2)}) collective-permute-start(f32[2,24,256]{2,1,0:T(8,128)S(1)} %get-tuple-element.14.field_ref), channel_id=1, source_target_pairs={{0,1},{1,0},{2,3},{3,2},{4,5},{5,4},{6,7},{7,6},{8,9},{9,8},{10,11... | collective-permute-start | bytes 147464 | tf_op jit(solution)/shard_map/ppermute | solution.py:266
  15.5 2.7 %collective-permute-start.4 = (f32[2,24,1]{2,1,0:T(8,128)S(1)}, f32[2,24,1]{2,1,0:T(8,128)S(1)}, u32[]{:S(2)}, u32[]{:S(2)}) collective-permute-start(f32[2,24,1]{2,1,0:T(8,128)S(1)} %slice_select_fusion), channel_id=1, source_target_pairs={{0,16},{16,0},{1,17},{17,1},{2,18},{18,2},{3,19},{19,3},{4,20},{20... | collective-permute-start | bytes 584 | tf_op jit(solution)/shard_map/ppermute | solution.py:246

commit v3 on v2

v3 whole, which is shorter than its diff:
```python
import functools
import jax
import jax.numpy as jnp
from jax import lax
from jax.experimental import pallas as pl
from jax.experimental.pallas import tpu as pltpu
from jax.sharding import PartitionSpec as P

NPHI = 32
NCHI = 32
layer_pitch = 2.0
F32 = jnp.float32
BF16 = jnp.bfloat16
VMEM = pl.BlockSpec(memory_space=pltpu.VMEM)
HBM = pl.BlockSpec(memory_space=pltpu.HBM)


def moments_body(order, sizes, count, is_first, is_last, pair, *refs):
    refs = list(refs)
    f_hbm = refs.pop(0)
    e_hbm = refs.pop(0) if is_first else None
    factors, early = (None, None) if is_first else (refs.pop(0), refs.pop(0))
    if is_last and pair:
        refs.pop(0)
    low_ref, high_ref = refs.pop(0), refs.pop(0)
    if is_first:
        factors = refs.pop(0)
    ahead = None if is_last else refs.pop(0)
    edge_ref = refs.pop(0) if is_last and pair else None
    buf, sem = refs.pop(0), refs.pop(0)
    rows, width = buf.shape[1:]
    angles, _, columns = f_hbm.shape
    here = high_ref.shape[0] // 3
    span = width // here
    blocks = columns // span
    deep = NCHI * 8
    per = 128 // NCHI
    pieces = angles // 128
    shifts = list(range(1, count)) + [0]
    me = lax.axis_index("angle")

    def columns_of(k):
        block = lax.rem(me + shifts[k], count)
        return pl.ds(pl.multiple_of(block * width, width), width)

    if is_first:
        ebuf, esem = refs.pop(0), refs.pop(0)
        exponent_copy = pltpu.make_async_copy(e_hbm, ebuf, esem)
        exponent_copy.start()
    held = 0 if is_first else early.shape[0]
    copies = []
    at = held
    for step, size in enumerate(sizes):
        copy = pltpu.make_async_copy(
            f_hbm.at[pl.ds(at, size), :, columns_of(order)],
            buf.at[pl.ds(at - held, size)],
            sem.at[step],
        )
        copy.start()
        copies.append((at, size, buf, at - held, copy))
        at += size
    if not is_first:
        copies.insert(0, (0, held, early, 0, None))
    if not is_last:
        asem = refs.pop(0)
        ahead_copy = pltpu.make_async_copy(
            f_hbm.at[pl.ds(0, ahead.shape[0]), :, columns_of(order + 1)], ahead, asem
        )
        ahead_copy.start()
    lane = lax.broadcasted_iota(jnp.int32, (8, deep), 1)
    diagonal = (lane & 7) == lax.broadcasted_iota(jnp.int32, (8, deep), 0)
    chi = ((lane >> 3).astype(F32) - 0.5 * (NCHI - 1)) / (0.5 * NCHI)
    chi_chi = chi * chi
    if is_first:
        source = lax.broadcasted_iota(jnp.int32, (128, deep), 0)
        target = lax.broadcasted_iota(jnp.int32, (128, deep), 1) >> 3
        picked = lax.broadcasted_iota(jnp.int32, (rows, rows * blocks), 0)
        natural = lax.broadcasted_iota(jnp.int32, (rows, rows * blocks), 1)
        select = []
        for k in range(count):
            block = lax.rem(me + shifts[k], count)
            for b in range(here):
                select.append((natural == picked * blocks + block * here + b).astype(F32))
        select = jnp.concatenate(select, 0).astype(BF16)
        exponent_copy.wait()
        factor = jnp.exp2(ebuf[...].reshape(rows * blocks, angles).astype(F32)).astype(BF16)
        factor = jnp.dot(select, factor, preferred_element_type=F32)
        factor = jnp.concatenate(
            [factor[:, c * 128 : (c + 1) * 128] for c in range(pieces)], 0
        ).astype(BF16)
        for part in range(per):
            one_hot = (source == target + NCHI * part).astype(F32).astype(BF16)
            factors[part] = jnp.dot(factor, one_hot, preferred_element_type=F32)
    first_phi = me * (angles // NCHI)
    for start, size, where, offset, copy in copies:
        if copy is not None:
            copy.wait()
        for r in range(rows // 8):
            at_rows = slice(r * 8, r * 8 + 8)
            for b in range(here):
                at_columns = slice(b * span, (b + 1) * span)
                left = []
                for g in range(start // NCHI, (start + size) // NCHI):
                    phi = ((first_phi + g).astype(F32) - 0.5 * (NPHI - 1)) / (0.5 * NPHI)
                    top = (((g // per) * count + order) * here + b) * rows + r * 8
                    unit = jnp.where(diagonal, factors[g % per, top : top + 8], 0.0)
                    left.append(
                        jnp.concatenate(
                            [
                                unit,
                                unit * phi,
                                unit * chi,
                                unit * (phi * phi),
                                unit * chi_chi,
                                unit * (phi * chi),
                            ],
                            0,
                        ).astype(BF16)
                    )
                left = jnp.concatenate(left, 1)
                cells = where[offset : offset + size, at_rows, at_columns].reshape(size * 8, span)
                sums = jnp.dot(left, cells, preferred_element_type=F32)
                for m in range(6):
                    value = sums[m * 8 : m * 8 + 8]
                    if m < 3:
                        if start:
                            value = value + low_ref[m, at_rows, at_columns]
                        low_ref[m, at_rows, at_columns] = value
                    else:
                        if start:
                            value = value + high_ref[(m - 3) * here + b, at_rows]
                        high_ref[(m - 3) * here + b, at_rows] = value
    if edge_ref is not None:
        column = lax.broadcasted_iota(jnp.int32, (rows, 128), 1)
        slab = jnp.zeros((rows, 128), F32)
        for m in range(3):
            edge = jnp.where(me == 0, low_ref[m, :, width - 1 :], low_ref[m, :, :1])
            slab = jnp.where(column == m, edge, slab)
        edge_ref[3 * here] = slab
    if not is_last:
        ahead_copy.wait()


def step_sizes(groups, most):
    sizes = []
    while groups:
        size = min(most, max(groups // 2, 1) if groups <= most else groups)
        sizes.append(size * NCHI)
        groups -= size
    return sizes


def all_moments(frames, exponents, count, pair):
    angles, rows, columns = frames.shape
    width = columns // count
    here = width * exponents.shape[1] // columns
    span = width // here
    low_shape = jax.ShapeDtypeStruct((3, rows, width), F32)
    high_shape = jax.ShapeDtypeStruct((3 * here, rows, span), F32)
    message = jax.ShapeDtypeStruct((3 * here + 1, rows, span), F32)
    factor_shape = jax.ShapeDtypeStruct(
        (128 // NCHI, angles // 128 * count * here * rows, NCHI * 8), F32
    )
    groups = angles // NCHI
    quarter = max(groups // 4, 1)
    held = quarter * NCHI
    early_shape = jax.ShapeDtypeStruct((held, rows, width), BF16)
    sent = []
    for k in range(count):
        is_first, is_last = k == 0, k == count - 1
        sizes = step_sizes(groups if is_first else groups - quarter, quarter)
        own = 0 if is_first else held
        operands, specs, out_shape, alias = [frames], [HBM], [], {}
        scratch = [
            pltpu.VMEM((angles - own, rows, width), BF16),
            pltpu.SemaphoreType.DMA((len(sizes),)),
        ]
        if is_first:
            operands += [exponents]
            specs += [HBM]
            scratch += [pltpu.VMEM(exponents.shape, jnp.int32), pltpu.SemaphoreType.DMA]
        else:
            operands += [factors, early]
            specs += [VMEM, VMEM]
        out_shape += [low_shape, message if pair and not is_last else high_shape]
        if is_first:
            out_shape += [factor_shape]
        if not is_last:
            out_shape += [early_shape]
            scratch += [pltpu.SemaphoreType.DMA]
        if is_last and pair:
            alias = {len(operands): len(out_shape)}
            operands += [sent[0][1]]
            specs += [VMEM]
            out_shape += [message]
        out = pl.pallas_call(
            functools.partial(moments_body, k, sizes, count, is_first, is_last, pair),
            out_shape=out_shape,
            in_specs=specs,
            out_specs=[VMEM] * len(out_shape),
            scratch_shapes=scratch,
            input_output_aliases=alias,
            name=f"moments_{k}",
            compiler_params=pltpu.CompilerParams(vmem_limit_bytes=28 << 20),
            cost_estimate=pl.CostEstimate(
                flops=512 * angles * rows * width,
                bytes_accessed=2 * angles * rows * width,
                transcendentals=0,
            ),
        )(*operands)
        low, high = out[:2]
        if is_first:
            factors = out[2]
        if not is_last:
            early = out[3 if is_first else 2]
            pairs = [(i, (i + k + 1) % count) for i in range(count)]
            moved = lax.ppermute(low, "angle", pairs)
            sent.append((low, high, moved, pairs))
    highs = [entry[1] for entry in sent]
    if pair:
        highs = [out[2]]
    moved_high = [lax.ppermute(h, "angle", entry[3]) for h, entry in zip(highs, sent)]
    return low, high, [entry[2] for entry in sent], moved_high, sent[0][0]


def field_body(count, own_ref, *refs):
    parts, (field_ref, even_ref, odd_ref) = refs[: count - 1], refs[count - 1 :]
    total = own_ref[...]
    for part in parts:
        total = total + part[...]
    first = total[1] / total[0]
    second = total[2] / total[0]
    field_ref[0] = first
    field_ref[1] = second
    rows = first.shape[0]
    is_even = lax.rem(lax.axis_index("tile"), 2) == 0
    for c, value in ((0, first), (1, second)):
        head, tail = value[:1], value[rows - 1 :]
        even_ref[c] = jnp.where(is_even, tail, head)
        odd_ref[c] = jnp.where(is_even, head, tail)


def field_of(own, parts):
    _, rows, width = own.shape
    edge = jax.ShapeDtypeStruct((2, 1, width), F32)
    return pl.pallas_call(
        functools.partial(field_body, len(parts) + 1),
        out_shape=[jax.ShapeDtypeStruct((2, rows, width), F32), edge, edge],
        in_specs=[VMEM] * (len(parts) + 1),
        out_specs=[VMEM] * 3,
        name="field",
        compiler_params=pltpu.CompilerParams(vmem_limit_bytes=4 << 20),
    )(own, *parts)


def spread_body(count, mask_ref, field_ref, low_ref, high_ref, *refs):
    parts, (orient_ref, spread_ref) = refs[: 2 * count - 2], refs[2 * count - 2 :]
    here = high_ref.shape[0] // 3
    span = high_ref.shape[2]
    for b in range(here):
        at = slice(b * span, (b + 1) * span)
        mask = mask_ref[0, :, at].astype(F32)
        zeroth = low_ref[0, :, at]
        seconds = [high_ref[m * here + b] for m in range(3)]
        for k in range(count - 1):
            zeroth = zeroth + parts[2 * k][0, :, at]
            seconds = [x + parts[2 * k + 1][m * here + b] for m, x in enumerate(seconds)]
        first, second = field_ref[0, :, at], field_ref[1, :, at]
        orient_ref[0, 0, :, at] = first * mask
        orient_ref[1, 0, :, at] = second * mask
        spread_ref[0, 0, :, at] = (seconds[0] / zeroth - first * first) * mask
        spread_ref[1, 0, :, at] = (seconds[1] / zeroth - second * second) * mask
        spread_ref[2, 0, :, at] = (seconds[2] / zeroth - first * second) * mask


def spread_of(mask, field, low, high, parts):
    _, rows, width = field.shape
    flat = [x for pair in parts for x in pair]
    return pl.pallas_call(
        functools.partial(spread_body, len(parts) + 1),
        out_shape=[
            jax.ShapeDtypeStruct((2, 1, rows, width), F32),
            jax.ShapeDtypeStruct((3, 1, rows, width), F32),
        ],
        in_specs=[VMEM] * (4 + len(flat)),
        out_specs=[VMEM] * 2,
        name="spread",
        compiler_params=pltpu.CompilerParams(vmem_limit_bytes=4 << 20),
    )(mask, field, low, high, *flat)


def nye_body(two_layers, pair, mask_ref, field_ref, even_ref, odd_ref, one_ref, two_ref, below_ref, above_ref, nye_ref):
    rows, width = field_ref.shape[1:]
    mask = mask_ref[0].astype(F32)
    tile, tiles = lax.axis_index("tile"), lax.axis_size("tile")
    is_even = lax.rem(tile, 2) == 0
    row = lax.broadcasted_iota(jnp.int32, (rows, width), 0)
    column = lax.broadcasted_iota(jnp.int32, (rows, width), 1)
    along_x, along_y, along_z = [], [], []
    if pair:
        is_left = lax.axis_index("angle") == 0
        here_sums = [
            jnp.where(is_left, one_ref[m, :, :1], one_ref[m, :, width - 1 :]) for m in range(3)
        ]
        sums = [x + two_ref[two_ref.shape[0] - 1, :, m : m + 1] for m, x in enumerate(here_sums)]
    for c in range(2):
        value = field_ref[c]
        upper = jnp.where(is_even, odd_ref[c], even_ref[c])
        lower = jnp.where(is_even, even_ref[c], odd_ref[c])
        upper = jnp.where(tile == 0, 0.0, upper)
        lower = jnp.where(tile == tiles - 1, 0.0, lower)
        before = jnp.where(row == 0, upper, pltpu.roll(value, 1, 0))
        after = jnp.where(row == rows - 1, lower, pltpu.roll(value, rows - 1, 0))
        along_y.append(0.5 * (after - before))
        if pair:
            edge = sums[c + 1] / sums[0]
            left, right = jnp.where(is_left, 0.0, edge), jnp.where(is_left, edge, 0.0)
        else:
            left, right = one_ref[c], two_ref[c]
        before = jnp.where(column == 0, left, pltpu.roll(value, 1, 1))
        after = jnp.where(column == width - 1, right, pltpu.roll(value, width - 1, 1))
        along_x.append(0.5 * (after - before))
        lower_layer, upper_layer = below_ref[c], above_ref[c]
        if two_layers:
            is_first = lax.axis_index("layer") == 0
            lower_layer = jnp.where(is_first, 0.0, lower_layer)
            upper_layer = jnp.where(is_first, upper_layer, 0.0)
        along_z.append((0.5 / layer_pitch) * (upper_layer - lower_layer))
    nye_ref[0, 0] = -along_y[1] * mask
    nye_ref[1, 0] = -along_x[0] * mask
    nye_ref[2, 0] = -(along_x[0] + along_y[1]) * mask
    nye_ref[3, 0] = along_x[1] * mask
    nye_ref[4, 0] = along_y[0] * mask
    nye_ref[5, 0] = along_z[0] * mask
    nye_ref[6, 0] = along_z[1] * mask


def nye_of(two_layers, pair, *operands):
    _, rows, width = operands[1].shape
    return pl.pallas_call(
        functools.partial(nye_body, two_layers, pair),
        out_shape=jax.ShapeDtypeStruct((7, 1, rows, width), F32),
        in_specs=[VMEM] * len(operands),
        out_specs=VMEM,
        name="nye",
        compiler_params=pltpu.CompilerParams(vmem_limit_bytes=4 << 20),
    )(*operands)


def rows_exchange(message, start):
    count, tiles = lax.axis_size("angle"), lax.axis_size("tile")
    pairs = []
    for a in range(count):
        for t in range(start, tiles - 1, 2):
            i = a * tiles + t
            pairs += [(i, i + 1), (i + 1, i)]
    used = {i for i, _ in pairs}
    for a in range(0, count - 1, 2):
        for t in range(tiles):
            i, j = a * tiles + t, (a + 1) * tiles + t
            if i not in used:
                pairs += [(i, j), (j, i)]
    return lax.ppermute(message, ("angle", "tile"), pairs)


def both_sides(tail, head, axis):
    count = lax.axis_size(axis)
    return (
        lax.ppermute(tail, axis, [(i, i + 1) for i in range(count - 1)]),
        lax.ppermute(head, axis, [(i + 1, i) for i in range(count - 1)]),
    )


def on_device(frames, exponents, valid_mask):
    count = lax.axis_size("angle")
    pair = count == 2
    frames = pltpu.with_memory_space_constraint(frames[0], pltpu.HBM)
    exponents = pltpu.with_memory_space_constraint(exponents[0].transpose(1, 2, 0), pltpu.HBM)
    low, high, lows, highs, near = all_moments(frames, exponents, count, pair)
    field, even, odd = field_of(low, lows)
    two_layers = lax.axis_size("layer") == 2
    if two_layers:
        below = above = lax.ppermute(field, "layer", [(0, 1), (1, 0)])
    else:
        below, above = both_sides(field, field, "layer")
    odd = rows_exchange(odd, 1)
    even = rows_exchange(even, 0)
    if pair:
        one, two = near, highs[0]
    else:
        one, two = both_sides(field[:, :, -1:], field[:, :, :1], "angle")
    orient, spread = spread_of(valid_mask, field, low, high, list(zip(lows, highs)))
    nye = nye_of(two_layers, pair, valid_mask, field, even, odd, one, two, below, above)
    return orient, spread, nye


def solution(mesh):
    in_specs = (
        P("layer", "angle", "tile", None),
        P("layer", "angle", "tile", None),
        P("layer", "tile", "angle"),
    )
    out_specs = (P(None, "layer", "tile", "angle"),) * 3
    return jax.shard_map(
        on_device, mesh=mesh, in_specs=in_specs, out_specs=out_specs, check_vma=False
    )
```

time: 19.2 us -> 17.1 us (0.89)
  the two profiles are of different devices: /device:TPU:1 before, /device:TPU:0 now
where the time goes in v3:
time: 17.1 us; the launch traced here: 16.9 us
  Pallas kernels  8.17 us (48%)
  starting transfers between devices  6.7 us (39%)
  waiting for transfers between devices  1.4 us (8%)
  between operations  0.66 us (4%)
    pallas_call x2, Pallas kernels, all_moments(): pl.pallas_call(functools.partial(moments_body, k, sizes, count, is_first,...  6.65 us
    ppermute x1, starting transfers between devices, all_moments(): moved = lax.ppermute(low, 'angle', pairs)  3.06 us
    ppermute x1, starting transfers between devices, on_device(): below = above = lax.ppermute(field, 'layer', [(0, 1), (1, 0)])  2.04 us
    ppermute x2, starting transfers between devices, rows_exchange(): return lax.ppermute(message, ('angle', 'tile'), pairs)  1.52 us
    ppermute x1, waiting for transfers between devices, all_moments(): lax.ppermute(h, 'angle', entry[3])  0.87 us
    pallas_call x1, Pallas kernels, nye_of(): pl.pallas_call(functools.partial(nye_body, two_layers, pair), out_shape=j...  0.83 us
    pallas_call x1, Pallas kernels, spread_of(): pl.pallas_call(functools.partial(spread_body, len(parts) + 1), out_shape=...  0.67 us
    ppermute x2, waiting for transfers between devices, rows_exchange(): return lax.ppermute(message, ('angle', 'tile'), pairs)  0.52 us
  transfers between devices with their start and end apart: 5, of which 2 were waited for; matrix products, arithmetic and copies ran while one was open for 0% of the time, Pallas kernels for 22%

profile of v3, /device:TPU:0, one launch (start us, length us, event | category | flops | bytes accessed | tf_op | source)
XLA Modules:
  0.0 16.9 jit_solution(16290620057560042771)
XLA Ops:
  0.6 3.6 %moments_0.1 = (f32[3,24,256]{2,1,0:T(8,128)S(1)}, f32[7,24,128]{2,1,0:T(8,128)S(1)}, f32[4,384,256]{2,1,0:T(8,128)S(1)}, bf16[128,24,256]{2,1,0:T(8,128)(2,1)S(1)}) custom-call(bf16[512,24,512]{2,1,0:T(8,128)(2,1)} %bitcast.4, s32[24,4,512]{2,1,0:T(4,128)} %bitcast.6), custom_call_target="tpu_custom_call" | custom-call | flops 1610612736 | bytes 6291456 | tf_op jit(solution)/shard_map/moments_0/pallas_call | solution.py:196
  4.2 3.1 %collective-permute-start = (f32[3,24,256]{2,1,0:T(8,128)S(1)}, f32[3,24,256]{2,1,0:T(8,128)S(1)}, u32[]{:S(2)}, u32[]{:S(2)}) collective-permute-start(f32[3,24,256]{2,1,0:T(8,128)S(1)} %get-tuple-element.19.one_ref), channel_id=1, source_target_pairs={{0,16},{16,0},{1,17},{17,1},{2,18},{18,2},{3,19},{19,3},{4,20},{20... | collective-permute-start | bytes 221192 | tf_op jit(solution)/shard_map/ppermute | solution.py:217
  7.3 0.0 copy-start
  7.3 3.1 %moments_1.1 = (f32[3,24,256]{2,1,0:T(8,128)S(1)}, f32[6,24,128]{2,1,0:T(8,128)S(1)}, f32[7,24,128]{2,1,0:T(8,128)S(1)}) custom-call(bf16[512,24,512]{2,1,0:T(8,128)(2,1)} %bitcast.5, f32[4,384,256]{2,1,0:T(8,128)S(1)} %get-tuple-element.15.refs_1_, bf16[128,24,256]{2,1,0:T(8,128)(2,1)S(1)} %get-tuple-element.16.refs_2_, ...), custom_call_target="tpu_custom_call", output_to_operand_aliasing={{2}: (3, {})} | custom-call | flops 1610612736 | bytes 6291456 | tf_op jit(solution)/shard_map/moments_1/pallas_call | solution.py:196
  10.4 0.1 collective-permute-start.1
  10.4 0.0 collective-permute-done.refs_0_
  10.5 2.0 %collective-permute-start.4 = (f32[2,24,256]{2,1,0:T(8,128)S(1)}, f32[2,24,256]{2,1,0:T(8,128)S(1)}, u32[]{:S(2)}, u32[]{:S(2)}) collective-permute-start(f32[2,24,256]{2,1,0:T(8,128)S(1)} %get-tuple-element.20.field_ref), channel_id=1, source_target_pairs={{0,1},{1,0},{2,3},{3,2},{4,5},{5,4},{6,7},{7,6},{8,9},{9,8},{10,11... | collective-permute-start | bytes 147464 | tf_op jit(solution)/shard_map/ppermute | solution.py:383
  12.5 0.0 collective-permute-start.2
  12.5 1.5 %collective-permute-start.3 = (f32[2,1,256]{2,1,0:T(1,128)S(1)}, f32[2,1,256]{2,1,0:T(1,128)S(1)}, u32[]{:S(2)}, u32[]{:S(2)}) collective-permute-start(f32[2,1,256]{2,1,0:T(1,128)S(1)} %get-tuple-element.26), channel_id=1, source_target_pairs={{2,4},{4,2},{6,8},{8,6},{10,12},{12,10},{18,20},{20,18},{22,24},{2... | collective-permute-start | bytes 6152 | tf_op jit(solution)/shard_map/ppermute | solution.py:363
  14.0 0.9 %collective-permute-done.1.refs_1_.two_ref = f32[7,24,128]{2,1,0:T(8,128)S(1)} collective-permute-done((f32[7,24,128]{2,1,0:T(8,128)S(1)}, f32[7,24,128]{2,1,0:T(8,128)S(1)}, u32[]{:S(2)}, u32[]{:S(2)}) %collective-permute-start.1) | collective-permute-done | bytes 86048 | tf_op jit(solution)/shard_map/ppermute | solution.py:222
  14.9 0.0 copy-done
  14.9 0.7 %spread.1 = (f32[2,1,24,256]{3,2,1,0:T(8,128)}, f32[3,1,24,256]{3,2,1,0:T(8,128)}) custom-call(s32[1,24,256]{2,1,0:T(8,128)S(1)} %copy-done, f32[2,24,256]{2,1,0:T(8,128)S(1)} %get-tuple-element.20.field_ref, f32[3,24,256]{2,1,0:T(8,128)S(1)} %get-tuple-element.18.own_ref.low_ref, f32[6,24,128]{2,1,0:T(8,128)S(1)} %get-tuple-element.21.high_ref, ...), custom_call_target="tpu_custom_call" | custom-call | tf_op jit(solution)/shard_map/spread/pallas_call | solution.py:279
  15.6 0.0 collective-permute-done.2.even_ref
  15.6 0.5 %collective-permute-done.3.odd_ref = f32[2,1,256]{2,1,0:T(1,128)S(1)} collective-permute-done((f32[2,1,256]{2,1,0:T(1,128)S(1)}, f32[2,1,256]{2,1,0:T(1,128)S(1)}, u32[]{:S(2)}, u32[]{:S(2)}) %collective-permute-start.3) | collective-permute-done | bytes 2080 | tf_op jit(solution)/shard_map/ppermute | solution.py:363
  16.1 0.0 collective-permute-done.4.below_ref.above_ref
  16.1 0.8 %nye.1 = f32[7,1,24,256]{3,2,1,0:T(8,128)} custom-call(s32[1,24,256]{2,1,0:T(8,128)S(1)} %copy-done, f32[2,24,256]{2,1,0:T(8,128)S(1)} %get-tuple-element.20.field_ref, f32[2,1,256]{2,1,0:T(1,128)S(1)} %collective-permute-done.2.even_ref, f32[2,1,256]{2,1,0:T(1,128)S(1)} %collective-permute-done.3.odd_ref, f32[3,24,256]{2,1,0:T(8,128)S(1)} %get-tuple-element.19.one_ref, ...), custom_call_target="tpu_custom_call" | custom-call | tf_op jit(solution)/shard_map/nye/pallas_call | solution.py:340
  (1 shorter events, 0.0 us)
Async XLA Ops:
  4.2 6.2 %collective-permute-start = (f32[3,24,256]{2,1,0:T(8,128)S(1)}, f32[3,24,256]{2,1,0:T(8,128)S(1)}, u32[]{:S(2)}, u32[]{:S(2)}) collective-permute-start(f32[3,24,256]{2,1,0:T(8,128)S(1)} %get-tuple-element.19.one_ref), channel_id=1, source_target_pairs={{0,16},{16,0},{1,17},{17,1},{2,18},{18,2},{3,19},{19,3},{4,20},{20... | collective-permute-start | bytes 221192 | tf_op jit(solution)/shard_map/ppermute | solution.py:217
  7.3 7.6 %copy-start = (s32[1,24,256]{2,1,0:T(8,128)S(1)}, s32[1,24,256]{2,1,0:T(8,128)}, u32[]{:S(2)}) copy-start(s32[1,24,256]{2,1,0:T(8,128)} %mask_ref.3) | copy-start | bytes 73732
  10.4 4.6 %collective-permute-start.1 = (f32[7,24,128]{2,1,0:T(8,128)S(1)}, f32[7,24,128]{2,1,0:T(8,128)S(1)}, u32[]{:S(2)}, u32[]{:S(2)}) collective-permute-start(f32[7,24,128]{2,1,0:T(8,128)S(1)} %get-tuple-element.22), channel_id=1, source_target_pairs={{0,16},{16,0},{1,17},{17,1},{2,18},{18,2},{3,19},{19,3},{4,20},{20... | collective-permute-start | bytes 258056 | tf_op jit(solution)/shard_map/ppermute | solution.py:222
  10.5 5.6 %collective-permute-start.4 = (f32[2,24,256]{2,1,0:T(8,128)S(1)}, f32[2,24,256]{2,1,0:T(8,128)S(1)}, u32[]{:S(2)}, u32[]{:S(2)}) collective-permute-start(f32[2,24,256]{2,1,0:T(8,128)S(1)} %get-tuple-element.20.field_ref), channel_id=1, source_target_pairs={{0,1},{1,0},{2,3},{3,2},{4,5},{5,4},{6,7},{7,6},{8,9},{9,8},{10,11... | collective-permute-start | bytes 147464 | tf_op jit(solution)/shard_map/ppermute | solution.py:383
  12.5 3.1 %collective-permute-start.2 = (f32[2,1,256]{2,1,0:T(1,128)S(1)}, f32[2,1,256]{2,1,0:T(1,128)S(1)}, u32[]{:S(2)}, u32[]{:S(2)}) collective-permute-start(f32[2,1,256]{2,1,0:T(1,128)S(1)} %get-tuple-element.25), channel_id=1, source_target_pairs={{0,2},{2,0},{4,6},{6,4},{8,10},{10,8},{12,14},{14,12},{16,18},{18,... | collective-permute-start | bytes 6152 | tf_op jit(solution)/shard_map/ppermute | solution.py:363
  12.5 3.6 %collective-permute-start.3 = (f32[2,1,256]{2,1,0:T(1,128)S(1)}, f32[2,1,256]{2,1,0:T(1,128)S(1)}, u32[]{:S(2)}, u32[]{:S(2)}) collective-permute-start(f32[2,1,256]{2,1,0:T(1,128)S(1)} %get-tuple-element.26), channel_id=1, source_target_pairs={{2,4},{4,2},{6,8},{8,6},{10,12},{12,10},{18,20},{20,18},{22,24},{2... | collective-permute-start | bytes 6152 | tf_op jit(solution)/shard_map/ppermute | solution.py:363

commit v4 on v3

--- a/solution.py
+++ b/solution.py
@@ -6,6 +6,7 @@
 from jax.experimental.pallas import tpu as pltpu
 from jax.sharding import PartitionSpec as P
 
+
 NPHI = 32
 NCHI = 32
 layer_pitch = 2.0
@@ -19,12 +20,12 @@
     refs = list(refs)
     f_hbm = refs.pop(0)
     e_hbm = refs.pop(0) if is_first else None
-    factors, early = (None, None) if is_first else (refs.pop(0), refs.pop(0))
+    ebuf, early = (None, None) if is_first else (refs.pop(0), refs.pop(0))
     if is_last and pair:
         refs.pop(0)
     low_ref, high_ref = refs.pop(0), refs.pop(0)
     if is_first:
-        factors = refs.pop(0)
+        ebuf = refs.pop(0)
     ahead = None if is_last else refs.pop(0)
     edge_ref = refs.pop(0) if is_last and pair else None
     buf, sem = refs.pop(0), refs.pop(0)
@@ -34,8 +35,7 @@
     span = width // here
     blocks = columns // span
     deep = NCHI * 8
-    per = 128 // NCHI
-    pieces = angles // 128
+    tiles = angles // 128
     shifts = list(range(1, count)) + [0]
     me = lax.axis_index("angle")
 
@@ -44,7 +44,7 @@
         return pl.ds(pl.multiple_of(block * width, width), width)
 
     if is_first:
-        ebuf, esem = refs.pop(0), refs.pop(0)
+        esem = refs.pop(0)
         exponent_copy = pltpu.make_async_copy(e_hbm, ebuf, esem)
         exponent_copy.start()
     held = 0 if is_first else early.shape[0]
@@ -72,64 +72,87 @@
     chi = ((lane >> 3).astype(F32) - 0.5 * (NCHI - 1)) / (0.5 * NCHI)
     chi_chi = chi * chi
     if is_first:
-        source = lax.broadcasted_iota(jnp.int32, (128, deep), 0)
-        target = lax.broadcasted_iota(jnp.int32, (128, deep), 1) >> 3
-        picked = lax.broadcasted_iota(jnp.int32, (rows, rows * blocks), 0)
-        natural = lax.broadcasted_iota(jnp.int32, (rows, rows * blocks), 1)
-        select = []
-        for k in range(count):
-            block = lax.rem(me + shifts[k], count)
-            for b in range(here):
-                select.append((natural == picked * blocks + block * here + b).astype(F32))
-        select = jnp.concatenate(select, 0).astype(BF16)
         exponent_copy.wait()
-        factor = jnp.exp2(ebuf[...].reshape(rows * blocks, angles).astype(F32)).astype(BF16)
-        factor = jnp.dot(select, factor, preferred_element_type=F32)
-        factor = jnp.concatenate(
-            [factor[:, c * 128 : (c + 1) * 128] for c in range(pieces)], 0
-        ).astype(BF16)
-        for part in range(per):
-            one_hot = (source == target + NCHI * part).astype(F32).astype(BF16)
-            factors[part] = jnp.dot(factor, one_hot, preferred_element_type=F32)
+    block = lax.rem(me + shifts[order], count)
+
+    def scales(b, tile):
+        top = tile * blocks + block * here + b
+        return jnp.exp2(ebuf[pl.ds(top, rows, stride=tiles * blocks), :].astype(F32))
+
+    scale_tiles = [[scales(b, tile) for tile in range(tiles)] for b in range(here)]
+    gather_lane = lax.broadcasted_iota(jnp.int32, (8, 128), 1) >> 3
+
+    def factor(b, r, g):
+        piece = scale_tiles[b][g * NCHI // 128][r * 8 : r * 8 + 8]
+        first = g * NCHI % 128
+        return jnp.concatenate(
+            [
+                jnp.take_along_axis(piece, gather_lane + (first + half * 16), axis=1)
+                for half in range(2)
+            ],
+            1,
+        )
+
     first_phi = me * (angles // NCHI)
-    for start, size, where, offset, copy in copies:
-        if copy is not None:
-            copy.wait()
+
+    def left_of(g, r):
+        phi = ((first_phi + g).astype(F32) - 0.5 * (NPHI - 1)) / (0.5 * NPHI)
+        left = []
+        for b in range(here):
+            unit = jnp.where(diagonal, factor(b, r, g), 0.0)
+            left += [
+                unit,
+                unit * phi,
+                unit * chi,
+                unit * (phi * phi),
+                unit * chi_chi,
+                unit * (phi * chi),
+            ]
+        return jnp.concatenate(left, 0).astype(BF16)
+
+    whole = rows // 8 // 2 * 2
+
+    def unit_of(g, r):
+        return r % 2 if r < whole else g % 2
+
+    keys = sorted({(unit_of(g, r), r) for g in range(angles // NCHI) for r in range(rows // 8)})
+
+    def accumulate(*flat):
+        sums = dict(zip(keys, flat))
+        turns = [0, 0]
+        for start, size, where, offset, copy in copies:
+            hoist = size <= 2 * NCHI
+            work = [
+                (g, r, left_of(g, r) if hoist else None)
+                for g in range(start // NCHI, (start + size) // NCHI)
+                for r in range(rows // 8)
+            ]
+            if copy is not None:
+                copy.wait()
+            for g, r, left in work:
+                first = offset + g * NCHI - start
+                cells = where[first : first + NCHI, r * 8 : r * 8 + 8, :].reshape(deep, width)
+                unit_index = unit_of(g, r)
+                stage = turns[unit_index] % 2
+                turns[unit_index] += 1
+                pltpu.matmul_push_rhs(cells, stage, unit_index)
+                left = left_of(g, r) if left is None else left
+                pltpu.matmul_acc_lhs(sums[unit_index, r], left, load_staged_rhs=stage)
         for r in range(rows // 8):
+            value = sum(pltpu.matmul_pop(sums[key]) for key in keys if key[1] == r)
             at_rows = slice(r * 8, r * 8 + 8)
             for b in range(here):
                 at_columns = slice(b * span, (b + 1) * span)
-                left = []
-                for g in range(start // NCHI, (start + size) // NCHI):
-                    phi = ((first_phi + g).astype(F32) - 0.5 * (NPHI - 1)) / (0.5 * NPHI)
-                    top = (((g // per) * count + order) * here + b) * rows + r * 8
-                    unit = jnp.where(diagonal, factors[g % per, top : top + 8], 0.0)
-                    left.append(
-                        jnp.concatenate(
-                            [
-                                unit,
-                                unit * phi,
-                                unit * chi,
-                                unit * (phi * phi),
-                                unit * chi_chi,
-                                unit * (phi * chi),
-                            ],
-                            0,
-                        ).astype(BF16)
-                    )
-                left = jnp.concatenate(left, 1)
-                cells = where[offset : offset + size, at_rows, at_columns].reshape(size * 8, span)
-                sums = jnp.dot(left, cells, preferred_element_type=F32)
                 for m in range(6):
-                    value = sums[m * 8 : m * 8 + 8]
+                    top = (b * 6 + m) * 8
+                    one = value[top : top + 8, at_columns]
                     if m < 3:
-                        if start:
-                            value = value + low_ref[m, at_rows, at_columns]
-                        low_ref[m, at_rows, at_columns] = value
+                        low_ref[m, at_rows, at_columns] = one
                     else:
-                        if start:
-                            value = value + high_ref[(m - 3) * here + b, at_rows]
-                        high_ref[(m - 3) * here + b, at_rows] = value
+                        high_ref[(m - 3) * here + b, at_rows] = one
+
+    accumulators = [pltpu.ACC(unit)((here * 48, width), F32) for unit, _ in keys]
+    pl.run_scoped(accumulate, *accumulators)
     if edge_ref is not None:
         column = lax.broadcasted_iota(jnp.int32, (rows, 128), 1)
         slab = jnp.zeros((rows, 128), F32)
@@ -153,22 +176,20 @@
 def all_moments(frames, exponents, count, pair):
     angles, rows, columns = frames.shape
     width = columns // count
-    here = width * exponents.shape[1] // columns
+    here = width * exponents.shape[0] * 128 // (columns * rows * angles)
     span = width // here
     low_shape = jax.ShapeDtypeStruct((3, rows, width), F32)
     high_shape = jax.ShapeDtypeStruct((3 * here, rows, span), F32)
     message = jax.ShapeDtypeStruct((3 * here + 1, rows, span), F32)
-    factor_shape = jax.ShapeDtypeStruct(
-        (128 // NCHI, angles // 128 * count * here * rows, NCHI * 8), F32
-    )
     groups = angles // NCHI
     quarter = max(groups // 4, 1)
-    held = quarter * NCHI
+    ahead_groups = max(groups // 4, 1)
+    held = ahead_groups * NCHI
     early_shape = jax.ShapeDtypeStruct((held, rows, width), BF16)
     sent = []
     for k in range(count):
         is_first, is_last = k == 0, k == count - 1
-        sizes = step_sizes(groups if is_first else groups - quarter, quarter)
+        sizes = step_sizes(groups if is_first else groups - ahead_groups, quarter)
         own = 0 if is_first else held
         operands, specs, out_shape, alias = [frames], [HBM], [], {}
         scratch = [
@@ -178,13 +199,13 @@
         if is_first:
             operands += [exponents]
             specs += [HBM]
-            scratch += [pltpu.VMEM(exponents.shape, jnp.int32), pltpu.SemaphoreType.DMA]
+            scratch += [pltpu.SemaphoreType.DMA]
         else:
-            operands += [factors, early]
+            operands += [held_exponents, early]
             specs += [VMEM, VMEM]
         out_shape += [low_shape, message if pair and not is_last else high_shape]
         if is_first:
-            out_shape += [factor_shape]
+            out_shape += [jax.ShapeDtypeStruct(exponents.shape, jnp.int32)]
         if not is_last:
             out_shape += [early_shape]
             scratch += [pltpu.SemaphoreType.DMA]
@@ -200,7 +221,6 @@
             out_specs=[VMEM] * len(out_shape),
             scratch_shapes=scratch,
             input_output_aliases=alias,
-            name=f"moments_{k}",
             compiler_params=pltpu.CompilerParams(vmem_limit_bytes=28 << 20),
             cost_estimate=pl.CostEstimate(
                 flops=512 * angles * rows * width,
@@ -210,7 +230,7 @@
         )(*operands)
         low, high = out[:2]
         if is_first:
-            factors = out[2]
+            held_exponents = out[2]
         if not is_last:
             early = out[3 if is_first else 2]
             pairs = [(i, (i + k + 1) % count) for i in range(count)]
@@ -253,8 +273,11 @@
     )(own, *parts)
 
 
-def spread_body(count, mask_ref, field_ref, low_ref, high_ref, *refs):
-    parts, (orient_ref, spread_ref) = refs[: 2 * count - 2], refs[2 * count - 2 :]
+def final_body(
+    count, two_layers, pair, mask_ref, field_ref, low_ref, high_ref, even_ref, odd_ref, one_ref, two_ref, below_ref, above_ref, *refs
+):
+    parts, (orient_ref, spread_ref, nye_ref) = refs[: 2 * count - 2], refs[2 * count - 2 :]
+    rows, width = field_ref.shape[1:]
     here = high_ref.shape[0] // 3
     span = high_ref.shape[2]
     for b in range(here):
@@ -271,26 +294,6 @@
         spread_ref[0, 0, :, at] = (seconds[0] / zeroth - first * first) * mask
         spread_ref[1, 0, :, at] = (seconds[1] / zeroth - second * second) * mask
         spread_ref[2, 0, :, at] = (seconds[2] / zeroth - first * second) * mask
-
-
-def spread_of(mask, field, low, high, parts):
-    _, rows, width = field.shape
-    flat = [x for pair in parts for x in pair]
-    return pl.pallas_call(
-        functools.partial(spread_body, len(parts) + 1),
-        out_shape=[
-            jax.ShapeDtypeStruct((2, 1, rows, width), F32),
-            jax.ShapeDtypeStruct((3, 1, rows, width), F32),
-        ],
-        in_specs=[VMEM] * (4 + len(flat)),
-        out_specs=[VMEM] * 2,
-        name="spread",
-        compiler_params=pltpu.CompilerParams(vmem_limit_bytes=4 << 20),
-    )(mask, field, low, high, *flat)
-
-
-def nye_body(two_layers, pair, mask_ref, field_ref, even_ref, odd_ref, one_ref, two_ref, below_ref, above_ref, nye_ref):
-    rows, width = field_ref.shape[1:]
     mask = mask_ref[0].astype(F32)
     tile, tiles = lax.axis_index("tile"), lax.axis_size("tile")
     is_even = lax.rem(tile, 2) == 0
@@ -335,32 +338,33 @@
     nye_ref[6, 0] = along_z[1] * mask
 
 
-def nye_of(two_layers, pair, *operands):
+def final_of(two_layers, pair, operands, parts):
     _, rows, width = operands[1].shape
+    flat = [x for both in parts for x in both]
     return pl.pallas_call(
-        functools.partial(nye_body, two_layers, pair),
-        out_shape=jax.ShapeDtypeStruct((7, 1, rows, width), F32),
-        in_specs=[VMEM] * len(operands),
-        out_specs=VMEM,
-        name="nye",
+        functools.partial(final_body, len(parts) + 1, two_layers, pair),
+        out_shape=[jax.ShapeDtypeStruct((n, 1, rows, width), F32) for n in (2, 3, 7)],
+        in_specs=[VMEM] * (len(operands) + len(flat)),
+        out_specs=[VMEM] * 3,
+        name="final",
         compiler_params=pltpu.CompilerParams(vmem_limit_bytes=4 << 20),
-    )(*operands)
+    )(*operands, *flat)
 
 
 def rows_exchange(message, start):
-    count, tiles = lax.axis_size("angle"), lax.axis_size("tile")
+    tiles, layers = lax.axis_size("tile"), lax.axis_size("layer")
     pairs = []
-    for a in range(count):
+    for j in range(layers):
         for t in range(start, tiles - 1, 2):
-            i = a * tiles + t
-            pairs += [(i, i + 1), (i + 1, i)]
+            i = t * layers + j
+            pairs += [(i, i + layers), (i + layers, i)]
     used = {i for i, _ in pairs}
-    for a in range(0, count - 1, 2):
-        for t in range(tiles):
-            i, j = a * tiles + t, (a + 1) * tiles + t
+    for t in range(tiles):
+        for j in range(0, layers - 1, 2):
+            i = t * layers + j
             if i not in used:
-                pairs += [(i, j), (j, i)]
-    return lax.ppermute(message, ("angle", "tile"), pairs)
+                pairs += [(i, i + 1), (i + 1, i)]
+    return lax.ppermute(message, ("tile", "layer"), pairs)
 
 
 def both_sides(tail, head, axis):
@@ -375,7 +379,10 @@
     count = lax.axis_size("angle")
     pair = count == 2
     frames = pltpu.with_memory_space_constraint(frames[0], pltpu.HBM)
-    exponents = pltpu.with_memory_space_constraint(exponents[0].transpose(1, 2, 0), pltpu.HBM)
+    angles, rows, blocks = exponents.shape[1:]
+    exponents = exponents[0].reshape(angles // 128, 128, rows, blocks).transpose(2, 0, 3, 1)
+    exponents = exponents.reshape(rows * angles // 128 * blocks, 128)
+    exponents = pltpu.with_memory_space_constraint(exponents, pltpu.HBM)
     low, high, lows, highs, near = all_moments(frames, exponents, count, pair)
     field, even, odd = field_of(low, lows)
     two_layers = lax.axis_size("layer") == 2
@@ -389,9 +396,8 @@
         one, two = near, highs[0]
     else:
         one, two = both_sides(field[:, :, -1:], field[:, :, :1], "angle")
-    orient, spread = spread_of(valid_mask, field, low, high, list(zip(lows, highs)))
-    nye = nye_of(two_layers, pair, valid_mask, field, even, odd, one, two, below, above)
-    return orient, spread, nye
+    operands = [valid_mask, field, low, high, even, odd, one, two, below, above]
+    return final_of(two_layers, pair, operands, list(zip(lows, highs)))
 
 
 def solution(mesh):
@@ -401,6 +407,12 @@
         P("layer", "tile", "angle"),
     )
     out_specs = (P(None, "layer", "tile", "angle"),) * 3
-    return jax.shard_map(
+    step = jax.shard_map(
         on_device, mesh=mesh, in_specs=in_specs, out_specs=out_specs, check_vma=False
     )
+
+    def whole(*arrays):
+        with jax.sharding.use_abstract_mesh(mesh.abstract_mesh):
+            return step(*arrays)
+
+    return whole

time: 17.1 us -> 16.9 us (0.988)
  waiting for transfers between devices: 1.4 us -> 3.44 us
  starting transfers between devices: 6.7 us -> 5.33 us
  Pallas kernels: 8.17 us -> 7.27 us
    ppermute x2, waiting for transfers between devices: 0.52 us -> 3.43 us  [rows_exchange(): return lax.ppermute(message, ('tile', 'layer'), pairs)]
    ppermute x2, starting transfers between devices: 1.52 us -> 0.16 us  [rows_exchange(): return lax.ppermute(message, ('tile', 'layer'), pairs)]
    ppermute x1, waiting for transfers between devices: 0.87 us -> 0.01 us  [all_moments(): lax.ppermute(h, 'angle', entry[3])]
    pallas_call x2 -> x1, Pallas kernels: 1.5 us -> 0.84 us  [final_of(): pl.pallas_call(functools.partial(final_body, len(parts) + 1, two_layers,...]
    pallas_call x2, Pallas kernels: 6.65 us -> 6.4 us  [all_moments(): pl.pallas_call(functools.partial(moments_body, k, sizes, count, is_first,...]
  transfers between devices with their start and end apart: 5 -> 5, of which waited for: 2 -> 2; matrix products, arithmetic and copies ran while one was open for 0% -> 0% of each run, Pallas kernels for 22% -> 18%
where the time goes in v4:
time: 16.9 us; the launch traced here: 16.7 us
  Pallas kernels  7.27 us (43%)
  starting transfers between devices  5.33 us (32%)
  waiting for transfers between devices  3.44 us (20%)
  between operations  0.67 us (4%)
    pallas_call x2, Pallas kernels, all_moments(): pl.pallas_call(functools.partial(moments_body, k, sizes, count, is_first,...  6.4 us
    ppermute x2, waiting for transfers between devices, rows_exchange(): return lax.ppermute(message, ('tile', 'layer'), pairs)  3.43 us
    ppermute x1, starting transfers between devices, all_moments(): moved = lax.ppermute(low, 'angle', pairs)  3.06 us
    ppermute x1, starting transfers between devices, on_device(): below = above = lax.ppermute(field, 'layer', [(0, 1), (1, 0)])  2.03 us
    pallas_call x1, Pallas kernels, final_of(): pl.pallas_call(functools.partial(final_body, len(parts) + 1, two_layers,...  0.84 us
  transfers between devices with their start and end apart: 5, of which 2 were waited for; matrix products, arithmetic and copies ran while one was open for 0% of the time, Pallas kernels for 18%

profile of v4, /device:TPU:0, one launch (start us, length us, event | category | flops | bytes accessed | tf_op | source)
XLA Modules:
  0.0 16.7 jit_solution(14246642769441422583)
XLA Ops:
  0.6 0.0 copy-start
  0.6 3.5 %shard_map.58 = (f32[3,24,256]{2,1,0:T(8,128)S(1)}, f32[7,24,128]{2,1,0:T(8,128)S(1)}, s32[384,128]{1,0:T(8,128)S(1)}, bf16[128,24,256]{2,1,0:T(8,128)(2,1)S(1)}) custom-call(bf16[512,24,512]{2,1,0:T(8,128)(2,1)} %bitcast.6, s32[384,128]{1,0:T(8,128)} %bitcast.8), custom_call_target="tpu_custom_call" | custom-call | flops 1610612736 | bytes 6291456 | tf_op jit(solution)/shard_map/pallas_call | solution.py:217
  4.1 3.1 %collective-permute-start = (f32[3,24,256]{2,1,0:T(8,128)S(1)}, f32[3,24,256]{2,1,0:T(8,128)S(1)}, u32[]{:S(2)}, u32[]{:S(2)}) collective-permute-start(f32[3,24,256]{2,1,0:T(8,128)S(1)} %get-tuple-element.17.one_ref), channel_id=1, source_target_pairs={{0,16},{16,0},{1,17},{17,1},{2,18},{18,2},{3,19},{19,3},{4,20},{20... | collective-permute-start | bytes 221192 | tf_op jit(solution)/shard_map/ppermute | solution.py:237
  7.2 2.9 %shard_map.59 = (f32[3,24,256]{2,1,0:T(8,128)S(1)}, f32[6,24,128]{2,1,0:T(8,128)S(1)}, f32[7,24,128]{2,1,0:T(8,128)S(1)}) custom-call(bf16[512,24,512]{2,1,0:T(8,128)(2,1)} %bitcast.7, s32[384,128]{1,0:T(8,128)S(1)} %get-tuple-element.13.refs_1_, bf16[128,24,256]{2,1,0:T(8,128)(2,1)S(1)} %get-tuple-element.14.refs_2_, ...), custom_call_target="tpu_custom_call", output_to_operand_aliasing={{2}: (3, {})} | custom-call | flops 1610612736 | bytes 6291456 | tf_op jit(solution)/shard_map/pallas_call | solution.py:217
  10.1 0.1 collective-permute-start.3
  10.2 0.0 collective-permute-done.refs_0_
  10.2 2.0 %collective-permute-start.4 = (f32[2,24,256]{2,1,0:T(8,128)S(1)}, f32[2,24,256]{2,1,0:T(8,128)S(1)}, u32[]{:S(2)}, u32[]{:S(2)}) collective-permute-start(f32[2,24,256]{2,1,0:T(8,128)S(1)} %get-tuple-element.18.field_ref), channel_id=1, source_target_pairs={{0,1},{1,0},{2,3},{3,2},{4,5},{5,4},{6,7},{7,6},{8,9},{9,8},{10,11... | collective-permute-start | bytes 147464 | tf_op jit(solution)/shard_map/ppermute | solution.py:390
  12.3 0.0 collective-permute-start.1
  12.3 0.2 collective-permute-start.2
  12.4 1.0 %collective-permute-done.1.even_ref = f32[2,1,256]{2,1,0:T(1,128)S(1)} collective-permute-done((f32[2,1,256]{2,1,0:T(1,128)S(1)}, f32[2,1,256]{2,1,0:T(1,128)S(1)}, u32[]{:S(2)}, u32[]{:S(2)}) %collective-permute-start.1) | collective-permute-done | bytes 2080 | tf_op jit(solution)/shard_map/ppermute | solution.py:367
  13.4 2.4 %collective-permute-done.2.odd_ref = f32[2,1,256]{2,1,0:T(1,128)S(1)} collective-permute-done((f32[2,1,256]{2,1,0:T(1,128)S(1)}, f32[2,1,256]{2,1,0:T(1,128)S(1)}, u32[]{:S(2)}, u32[]{:S(2)}) %collective-permute-start.2) | collective-permute-done | bytes 2080 | tf_op jit(solution)/shard_map/ppermute | solution.py:367
  15.9 0.0 collective-permute-done.3.two_ref.refs_1_
  15.9 0.0 collective-permute-done.4.below_ref.above_ref
  15.9 0.0 copy-done
  15.9 0.8 %final.1 = (f32[2,1,24,256]{3,2,1,0:T(8,128)}, f32[3,1,24,256]{3,2,1,0:T(8,128)}, f32[7,1,24,256]{3,2,1,0:T(8,128)}) custom-call(s32[1,24,256]{2,1,0:T(8,128)S(1)} %copy-done, f32[2,24,256]{2,1,0:T(8,128)S(1)} %get-tuple-element.18.field_ref, f32[3,24,256]{2,1,0:T(8,128)S(1)} %get-tuple-element.16.own_ref.low_ref, ...), custom_call_target="tpu_custom_call" | custom-call | tf_op jit(solution)/shard_map/final/pallas_call | solution.py:344
  (1 shorter events, 0.0 us)
Async XLA Ops:
  0.6 15.2 %copy-start = (s32[1,24,256]{2,1,0:T(8,128)S(1)}, s32[1,24,256]{2,1,0:T(8,128)}, u32[]{:S(2)}) copy-start(s32[1,24,256]{2,1,0:T(8,128)} %mask_ref.1) | copy-start | bytes 73732
  4.1 6.1 %collective-permute-start = (f32[3,24,256]{2,1,0:T(8,128)S(1)}, f32[3,24,256]{2,1,0:T(8,128)S(1)}, u32[]{:S(2)}, u32[]{:S(2)}) collective-permute-start(f32[3,24,256]{2,1,0:T(8,128)S(1)} %get-tuple-element.17.one_ref), channel_id=1, source_target_pairs={{0,16},{16,0},{1,17},{17,1},{2,18},{18,2},{3,19},{19,3},{4,20},{20... | collective-permute-start | bytes 221192 | tf_op jit(solution)/shard_map/ppermute | solution.py:237
  10.1 5.7 %collective-permute-start.3 = (f32[7,24,128]{2,1,0:T(8,128)S(1)}, f32[7,24,128]{2,1,0:T(8,128)S(1)}, u32[]{:S(2)}, u32[]{:S(2)}) collective-permute-start(f32[7,24,128]{2,1,0:T(8,128)S(1)} %get-tuple-element.22), channel_id=1, source_target_pairs={{0,16},{16,0},{1,17},{17,1},{2,18},{18,2},{3,19},{19,3},{4,20},{20... | collective-permute-start | bytes 258056 | tf_op jit(solution)/shard_map/ppermute | solution.py:242
  10.2 5.6 %collective-permute-start.4 = (f32[2,24,256]{2,1,0:T(8,128)S(1)}, f32[2,24,256]{2,1,0:T(8,128)S(1)}, u32[]{:S(2)}, u32[]{:S(2)}) collective-permute-start(f32[2,24,256]{2,1,0:T(8,128)S(1)} %get-tuple-element.18.field_ref), channel_id=1, source_target_pairs={{0,1},{1,0},{2,3},{3,2},{4,5},{5,4},{6,7},{7,6},{8,9},{9,8},{10,11... | collective-permute-start | bytes 147464 | tf_op jit(solution)/shard_map/ppermute | solution.py:390
  12.3 1.2 %collective-permute-start.1 = (f32[2,1,256]{2,1,0:T(1,128)S(1)}, f32[2,1,256]{2,1,0:T(1,128)S(1)}, u32[]{:S(2)}, u32[]{:S(2)}) collective-permute-start(f32[2,1,256]{2,1,0:T(1,128)S(1)} %get-tuple-element.20), channel_id=1, source_target_pairs={{0,2},{2,0},{4,6},{6,4},{8,10},{10,8},{12,14},{14,12},{1,3},{3,1},... | collective-permute-start | bytes 6152 | tf_op jit(solution)/shard_map/ppermute | solution.py:367
  12.3 3.6 %collective-permute-start.2 = (f32[2,1,256]{2,1,0:T(1,128)S(1)}, f32[2,1,256]{2,1,0:T(1,128)S(1)}, u32[]{:S(2)}, u32[]{:S(2)}) collective-permute-start(f32[2,1,256]{2,1,0:T(1,128)S(1)} %get-tuple-element.21), channel_id=1, source_target_pairs={{2,4},{4,2},{6,8},{8,6},{10,12},{12,10},{3,5},{5,3},{7,9},{9,7},{1... | collective-permute-start | bytes 6152 | tf_op jit(solution)/shard_map/ppermute | solution.py:367

commit v5 on v4

--- a/solution.py
+++ b/solution.py
@@ -77,7 +77,8 @@
 
     def scales(b, tile):
         top = tile * blocks + block * here + b
-        return jnp.exp2(ebuf[pl.ds(top, rows, stride=tiles * blocks), :].astype(F32))
+        exponent = ebuf[pl.ds(top, rows, stride=tiles * blocks), :]
+        return jnp.exp2(exponent.astype(F32)).astype(BF16).astype(F32)
 
     scale_tiles = [[scales(b, tile) for tile in range(tiles)] for b in range(here)]
     gather_lane = lax.broadcasted_iota(jnp.int32, (8, 128), 1) >> 3
@@ -167,7 +168,7 @@
 def step_sizes(groups, most):
     sizes = []
     while groups:
-        size = min(most, max(groups // 2, 1) if groups <= most else groups)
+        size = most if groups > most else max(groups // 2, min(groups, 2))
         sizes.append(size * NCHI)
         groups -= size
     return sizes

time: 16.9 us -> 16.8 us (level)
  no operation moved by 1% of the time
where the time goes in v5:
time: 16.8 us; the launch traced here: 16.7 us
  Pallas kernels  7.23 us (43%)
  starting transfers between devices  5.34 us (32%)
  waiting for transfers between devices  3.44 us (20%)
  between operations  0.67 us (4%)
    pallas_call x2, Pallas kernels, all_moments(): pl.pallas_call(functools.partial(moments_body, k, sizes, count, is_first,...  6.37 us
    ppermute x2, waiting for transfers between devices, rows_exchange(): return lax.ppermute(message, ('tile', 'layer'), pairs)  3.43 us
    ppermute x1, starting transfers between devices, all_moments(): moved = lax.ppermute(low, 'angle', pairs)  3.06 us
    ppermute x1, starting transfers between devices, on_device(): below = above = lax.ppermute(field, 'layer', [(0, 1), (1, 0)])  2.04 us
    pallas_call x1, Pallas kernels, final_of(): pl.pallas_call(functools.partial(final_body, len(parts) + 1, two_layers,...  0.84 us
  transfers between devices with their start and end apart: 5, of which 2 were waited for; matrix products, arithmetic and copies ran while one was open for 0% of the time, Pallas kernels for 18%

profile of v5, /device:TPU:0, one launch (start us, length us, event | category | flops | bytes accessed | tf_op | source)
XLA Modules:
  0.0 16.7 jit_solution(4330974055504386515)
XLA Ops:
  0.6 0.0 copy-start
  0.6 3.5 %shard_map.58 = (f32[3,24,256]{2,1,0:T(8,128)S(1)}, f32[7,24,128]{2,1,0:T(8,128)S(1)}, s32[384,128]{1,0:T(8,128)S(1)}, bf16[128,24,256]{2,1,0:T(8,128)(2,1)S(1)}) custom-call(bf16[512,24,512]{2,1,0:T(8,128)(2,1)} %bitcast.6, s32[384,128]{1,0:T(8,128)} %bitcast.8), custom_call_target="tpu_custom_call" | custom-call | flops 1610612736 | bytes 6291456 | tf_op jit(solution)/shard_map/pallas_call | solution.py:218
  4.1 3.1 %collective-permute-start = (f32[3,24,256]{2,1,0:T(8,128)S(1)}, f32[3,24,256]{2,1,0:T(8,128)S(1)}, u32[]{:S(2)}, u32[]{:S(2)}) collective-permute-start(f32[3,24,256]{2,1,0:T(8,128)S(1)} %get-tuple-element.17.one_ref), channel_id=1, source_target_pairs={{0,16},{16,0},{1,17},{17,1},{2,18},{18,2},{3,19},{19,3},{4,20},{20... | collective-permute-start | bytes 221192 | tf_op jit(solution)/shard_map/ppermute | solution.py:238
  7.2 2.9 %shard_map.59 = (f32[3,24,256]{2,1,0:T(8,128)S(1)}, f32[6,24,128]{2,1,0:T(8,128)S(1)}, f32[7,24,128]{2,1,0:T(8,128)S(1)}) custom-call(bf16[512,24,512]{2,1,0:T(8,128)(2,1)} %bitcast.7, s32[384,128]{1,0:T(8,128)S(1)} %get-tuple-element.13.refs_1_, bf16[128,24,256]{2,1,0:T(8,128)(2,1)S(1)} %get-tuple-element.14.refs_2_, ...), custom_call_target="tpu_custom_call", output_to_operand_aliasing={{2}: (3, {})} | custom-call | flops 1610612736 | bytes 6291456 | tf_op jit(solution)/shard_map/pallas_call | solution.py:218
  10.1 0.1 collective-permute-start.3
  10.2 0.0 collective-permute-done.refs_0_
  10.2 2.0 %collective-permute-start.4 = (f32[2,24,256]{2,1,0:T(8,128)S(1)}, f32[2,24,256]{2,1,0:T(8,128)S(1)}, u32[]{:S(2)}, u32[]{:S(2)}) collective-permute-start(f32[2,24,256]{2,1,0:T(8,128)S(1)} %get-tuple-element.18.field_ref), channel_id=1, source_target_pairs={{0,1},{1,0},{2,3},{3,2},{4,5},{5,4},{6,7},{7,6},{8,9},{9,8},{10,11... | collective-permute-start | bytes 147464 | tf_op jit(solution)/shard_map/ppermute | solution.py:391
  12.2 0.0 collective-permute-start.1
  12.2 0.2 collective-permute-start.2
  12.4 1.0 %collective-permute-done.1.even_ref = f32[2,1,256]{2,1,0:T(1,128)S(1)} collective-permute-done((f32[2,1,256]{2,1,0:T(1,128)S(1)}, f32[2,1,256]{2,1,0:T(1,128)S(1)}, u32[]{:S(2)}, u32[]{:S(2)}) %collective-permute-start.1) | collective-permute-done | bytes 2080 | tf_op jit(solution)/shard_map/ppermute | solution.py:368
  13.4 2.4 %collective-permute-done.2.odd_ref = f32[2,1,256]{2,1,0:T(1,128)S(1)} collective-permute-done((f32[2,1,256]{2,1,0:T(1,128)S(1)}, f32[2,1,256]{2,1,0:T(1,128)S(1)}, u32[]{:S(2)}, u32[]{:S(2)}) %collective-permute-start.2) | collective-permute-done | bytes 2080 | tf_op jit(solution)/shard_map/ppermute | solution.py:368
  15.8 0.0 collective-permute-done.3.two_ref.refs_1_
  15.8 0.0 collective-permute-done.4.below_ref.above_ref
  15.8 0.0 copy-done
  15.8 0.8 %final.1 = (f32[2,1,24,256]{3,2,1,0:T(8,128)}, f32[3,1,24,256]{3,2,1,0:T(8,128)}, f32[7,1,24,256]{3,2,1,0:T(8,128)}) custom-call(s32[1,24,256]{2,1,0:T(8,128)S(1)} %copy-done, f32[2,24,256]{2,1,0:T(8,128)S(1)} %get-tuple-element.18.field_ref, f32[3,24,256]{2,1,0:T(8,128)S(1)} %get-tuple-element.16.own_ref.low_ref, ...), custom_call_target="tpu_custom_call" | custom-call | tf_op jit(solution)/shard_map/final/pallas_call | solution.py:345
  (1 shorter events, 0.0 us)
Async XLA Ops:
  0.6 15.2 %copy-start = (s32[1,24,256]{2,1,0:T(8,128)S(1)}, s32[1,24,256]{2,1,0:T(8,128)}, u32[]{:S(2)}) copy-start(s32[1,24,256]{2,1,0:T(8,128)} %mask_ref.1) | copy-start | bytes 73732
  4.1 6.1 %collective-permute-start = (f32[3,24,256]{2,1,0:T(8,128)S(1)}, f32[3,24,256]{2,1,0:T(8,128)S(1)}, u32[]{:S(2)}, u32[]{:S(2)}) collective-permute-start(f32[3,24,256]{2,1,0:T(8,128)S(1)} %get-tuple-element.17.one_ref), channel_id=1, source_target_pairs={{0,16},{16,0},{1,17},{17,1},{2,18},{18,2},{3,19},{19,3},{4,20},{20... | collective-permute-start | bytes 221192 | tf_op jit(solution)/shard_map/ppermute | solution.py:238
  10.1 5.7 %collective-permute-start.3 = (f32[7,24,128]{2,1,0:T(8,128)S(1)}, f32[7,24,128]{2,1,0:T(8,128)S(1)}, u32[]{:S(2)}, u32[]{:S(2)}) collective-permute-start(f32[7,24,128]{2,1,0:T(8,128)S(1)} %get-tuple-element.22), channel_id=1, source_target_pairs={{0,16},{16,0},{1,17},{17,1},{2,18},{18,2},{3,19},{19,3},{4,20},{20... | collective-permute-start | bytes 258056 | tf_op jit(solution)/shard_map/ppermute | solution.py:243
  10.2 5.6 %collective-permute-start.4 = (f32[2,24,256]{2,1,0:T(8,128)S(1)}, f32[2,24,256]{2,1,0:T(8,128)S(1)}, u32[]{:S(2)}, u32[]{:S(2)}) collective-permute-start(f32[2,24,256]{2,1,0:T(8,128)S(1)} %get-tuple-element.18.field_ref), channel_id=1, source_target_pairs={{0,1},{1,0},{2,3},{3,2},{4,5},{5,4},{6,7},{7,6},{8,9},{9,8},{10,11... | collective-permute-start | bytes 147464 | tf_op jit(solution)/shard_map/ppermute | solution.py:391
  12.2 1.2 %collective-permute-start.1 = (f32[2,1,256]{2,1,0:T(1,128)S(1)}, f32[2,1,256]{2,1,0:T(1,128)S(1)}, u32[]{:S(2)}, u32[]{:S(2)}) collective-permute-start(f32[2,1,256]{2,1,0:T(1,128)S(1)} %get-tuple-element.20), channel_id=1, source_target_pairs={{0,2},{2,0},{4,6},{6,4},{8,10},{10,8},{12,14},{14,12},{1,3},{3,1},... | collective-permute-start | bytes 6152 | tf_op jit(solution)/shard_map/ppermute | solution.py:368
  12.2 3.6 %collective-permute-start.2 = (f32[2,1,256]{2,1,0:T(1,128)S(1)}, f32[2,1,256]{2,1,0:T(1,128)S(1)}, u32[]{:S(2)}, u32[]{:S(2)}) collective-permute-start(f32[2,1,256]{2,1,0:T(1,128)S(1)} %get-tuple-element.21), channel_id=1, source_target_pairs={{2,4},{4,2},{6,8},{8,6},{10,12},{12,10},{3,5},{5,3},{7,9},{9,7},{1... | collective-permute-start | bytes 6152 | tf_op jit(solution)/shard_map/ppermute | solution.py:368

commit v6 on v5

--- a/solution.py
+++ b/solution.py
@@ -277,8 +277,16 @@
 def final_body(
     count, two_layers, pair, mask_ref, field_ref, low_ref, high_ref, even_ref, odd_ref, one_ref, two_ref, below_ref, above_ref, *refs
 ):
-    parts, (orient_ref, spread_ref, nye_ref) = refs[: 2 * count - 2], refs[2 * count - 2 :]
+    parts, refs = refs[: 2 * count - 2], refs[2 * count - 2 :]
+    orient_out, spread_out, nye_out, orient_ref, spread_ref, nye_ref, sem = refs
     rows, width = field_ref.shape[1:]
+    copies = []
+
+    def send(source, target):
+        copy = pltpu.make_async_copy(source, target, sem.at[len(copies)])
+        copy.start()
+        copies.append(copy)
+
     here = high_ref.shape[0] // 3
     span = high_ref.shape[2]
     for b in range(here):
@@ -295,12 +303,22 @@
         spread_ref[0, 0, :, at] = (seconds[0] / zeroth - first * first) * mask
         spread_ref[1, 0, :, at] = (seconds[1] / zeroth - second * second) * mask
         spread_ref[2, 0, :, at] = (seconds[2] / zeroth - first * second) * mask
+    send(orient_ref, orient_out)
+    send(spread_ref, spread_out)
     mask = mask_ref[0].astype(F32)
+    for c in range(2):
+        lower_layer, upper_layer = below_ref[c], above_ref[c]
+        if two_layers:
+            is_first = lax.axis_index("layer") == 0
+            lower_layer = jnp.where(is_first, 0.0, lower_layer)
+            upper_layer = jnp.where(is_first, upper_layer, 0.0)
+        nye_ref[5 + c, 0] = (0.5 / layer_pitch) * (upper_layer - lower_layer) * mask
+    send(nye_ref.at[pl.ds(5, 2)], nye_out.at[pl.ds(5, 2)])
     tile, tiles = lax.axis_index("tile"), lax.axis_size("tile")
     is_even = lax.rem(tile, 2) == 0
     row = lax.broadcasted_iota(jnp.int32, (rows, width), 0)
     column = lax.broadcasted_iota(jnp.int32, (rows, width), 1)
-    along_x, along_y, along_z = [], [], []
+    along_x, along_y = [], []
     if pair:
         is_left = lax.axis_index("angle") == 0
         here_sums = [
@@ -324,19 +342,14 @@
         before = jnp.where(column == 0, left, pltpu.roll(value, 1, 1))
         after = jnp.where(column == width - 1, right, pltpu.roll(value, width - 1, 1))
         along_x.append(0.5 * (after - before))
-        lower_layer, upper_layer = below_ref[c], above_ref[c]
-        if two_layers:
-            is_first = lax.axis_index("layer") == 0
-            lower_layer = jnp.where(is_first, 0.0, lower_layer)
-            upper_layer = jnp.where(is_first, upper_layer, 0.0)
-        along_z.append((0.5 / layer_pitch) * (upper_layer - lower_layer))
     nye_ref[0, 0] = -along_y[1] * mask
     nye_ref[1, 0] = -along_x[0] * mask
     nye_ref[2, 0] = -(along_x[0] + along_y[1]) * mask
     nye_ref[3, 0] = along_x[1] * mask
     nye_ref[4, 0] = along_y[0] * mask
-    nye_ref[5, 0] = along_z[0] * mask
-    nye_ref[6, 0] = along_z[1] * mask
+    send(nye_ref.at[pl.ds(0, 5)], nye_out.at[pl.ds(0, 5)])
+    for copy in copies:
+        copy.wait()
 
 
 def final_of(two_layers, pair, operands, parts):
@@ -346,7 +359,9 @@
         functools.partial(final_body, len(parts) + 1, two_layers, pair),
         out_shape=[jax.ShapeDtypeStruct((n, 1, rows, width), F32) for n in (2, 3, 7)],
         in_specs=[VMEM] * (len(operands) + len(flat)),
-        out_specs=[VMEM] * 3,
+        out_specs=[HBM] * 3,
+        scratch_shapes=[pltpu.VMEM((n, 1, rows, width), F32) for n in (2, 3, 7)]
+        + [pltpu.SemaphoreType.DMA((4,))],
         name="final",
         compiler_params=pltpu.CompilerParams(vmem_limit_bytes=4 << 20),
     )(*operands, *flat)

time: 16.8 us -> 16.9 us (level)
  no operation moved by 1% of the time
where the time goes in v6:
time: 16.9 us; the launch traced here: 16.7 us
  Pallas kernels  7.25 us (43%)
  starting transfers between devices  5.34 us (32%)
  waiting for transfers between devices  3.44 us (20%)
  between operations  0.67 us (4%)
    pallas_call x2, Pallas kernels, all_moments(): pl.pallas_call(functools.partial(moments_body, k, sizes, count, is_first,...  6.37 us
    ppermute x2, waiting for transfers between devices, rows_exchange(): return lax.ppermute(message, ('tile', 'layer'), pairs)  3.43 us
    ppermute x1, starting transfers between devices, all_moments(): moved = lax.ppermute(low, 'angle', pairs)  3.06 us
    ppermute x1, starting transfers between devices, on_device(): below = above = lax.ppermute(field, 'layer', [(0, 1), (1, 0)])  2.04 us
    pallas_call x1, Pallas kernels, final_of(): pl.pallas_call(functools.partial(final_body, len(parts) + 1, two_layers,...  0.85 us
  transfers between devices with their start and end apart: 5, of which 2 were waited for; matrix products, arithmetic and copies ran while one was open for 0% of the time, Pallas kernels for 18%

profile of v6, /device:TPU:0, one launch (start us, length us, event | category | flops | bytes accessed | tf_op | source)
XLA Modules:
  0.0 16.7 jit_solution(3376049742144952881)
XLA Ops:
  0.6 0.0 copy-start
  0.6 3.5 %shard_map.58 = (f32[3,24,256]{2,1,0:T(8,128)S(1)}, f32[7,24,128]{2,1,0:T(8,128)S(1)}, s32[384,128]{1,0:T(8,128)S(1)}, bf16[128,24,256]{2,1,0:T(8,128)(2,1)S(1)}) custom-call(bf16[512,24,512]{2,1,0:T(8,128)(2,1)} %bitcast.6, s32[384,128]{1,0:T(8,128)} %bitcast.8), custom_call_target="tpu_custom_call" | custom-call | flops 1610612736 | bytes 6291456 | tf_op jit(solution)/shard_map/pallas_call | solution.py:218
  4.1 3.1 %collective-permute-start = (f32[3,24,256]{2,1,0:T(8,128)S(1)}, f32[3,24,256]{2,1,0:T(8,128)S(1)}, u32[]{:S(2)}, u32[]{:S(2)}) collective-permute-start(f32[3,24,256]{2,1,0:T(8,128)S(1)} %get-tuple-element.17.one_ref), channel_id=1, source_target_pairs={{0,16},{16,0},{1,17},{17,1},{2,18},{18,2},{3,19},{19,3},{4,20},{20... | collective-permute-start | bytes 221192 | tf_op jit(solution)/shard_map/ppermute | solution.py:238
  7.2 2.9 %shard_map.59 = (f32[3,24,256]{2,1,0:T(8,128)S(1)}, f32[6,24,128]{2,1,0:T(8,128)S(1)}, f32[7,24,128]{2,1,0:T(8,128)S(1)}) custom-call(bf16[512,24,512]{2,1,0:T(8,128)(2,1)} %bitcast.7, s32[384,128]{1,0:T(8,128)S(1)} %get-tuple-element.13.refs_1_, bf16[128,24,256]{2,1,0:T(8,128)(2,1)S(1)} %get-tuple-element.14.refs_2_, ...), custom_call_target="tpu_custom_call", output_to_operand_aliasing={{2}: (3, {})} | custom-call | flops 1610612736 | bytes 6291456 | tf_op jit(solution)/shard_map/pallas_call | solution.py:218
  10.1 0.1 collective-permute-start.3
  10.2 0.0 collective-permute-done.refs_0_
  10.2 2.0 %collective-permute-start.4 = (f32[2,24,256]{2,1,0:T(8,128)S(1)}, f32[2,24,256]{2,1,0:T(8,128)S(1)}, u32[]{:S(2)}, u32[]{:S(2)}) collective-permute-start(f32[2,24,256]{2,1,0:T(8,128)S(1)} %get-tuple-element.18.field_ref), channel_id=1, source_target_pairs={{0,1},{1,0},{2,3},{3,2},{4,5},{5,4},{6,7},{7,6},{8,9},{9,8},{10,11... | collective-permute-start | bytes 147464 | tf_op jit(solution)/shard_map/ppermute | solution.py:406
  12.2 0.0 collective-permute-start.1
  12.2 0.2 collective-permute-start.2
  12.4 1.0 %collective-permute-done.1.even_ref = f32[2,1,256]{2,1,0:T(1,128)S(1)} collective-permute-done((f32[2,1,256]{2,1,0:T(1,128)S(1)}, f32[2,1,256]{2,1,0:T(1,128)S(1)}, u32[]{:S(2)}, u32[]{:S(2)}) %collective-permute-start.1) | collective-permute-done | bytes 2080 | tf_op jit(solution)/shard_map/ppermute | solution.py:383
  13.4 2.4 %collective-permute-done.2.odd_ref = f32[2,1,256]{2,1,0:T(1,128)S(1)} collective-permute-done((f32[2,1,256]{2,1,0:T(1,128)S(1)}, f32[2,1,256]{2,1,0:T(1,128)S(1)}, u32[]{:S(2)}, u32[]{:S(2)}) %collective-permute-start.2) | collective-permute-done | bytes 2080 | tf_op jit(solution)/shard_map/ppermute | solution.py:383
  15.8 0.0 collective-permute-done.3.two_ref.refs_1_
  15.8 0.0 collective-permute-done.4.below_ref.above_ref
  15.8 0.0 copy-done
  15.8 0.9 %final.1 = (f32[2,1,24,256]{3,2,1,0:T(8,128)}, f32[3,1,24,256]{3,2,1,0:T(8,128)}, f32[7,1,24,256]{3,2,1,0:T(8,128)}) custom-call(s32[1,24,256]{2,1,0:T(8,128)S(1)} %copy-done, f32[2,24,256]{2,1,0:T(8,128)S(1)} %get-tuple-element.18.field_ref, f32[3,24,256]{2,1,0:T(8,128)S(1)} %get-tuple-element.16.own_ref.low_ref, ...), custom_call_target="tpu_custom_call" | custom-call | tf_op jit(solution)/shard_map/final/pallas_call | solution.py:358
  (1 shorter events, 0.0 us)
Async XLA Ops:
  0.6 15.2 %copy-start = (s32[1,24,256]{2,1,0:T(8,128)S(1)}, s32[1,24,256]{2,1,0:T(8,128)}, u32[]{:S(2)}) copy-start(s32[1,24,256]{2,1,0:T(8,128)} %mask_ref.1) | copy-start | bytes 73732
  4.1 6.1 %collective-permute-start = (f32[3,24,256]{2,1,0:T(8,128)S(1)}, f32[3,24,256]{2,1,0:T(8,128)S(1)}, u32[]{:S(2)}, u32[]{:S(2)}) collective-permute-start(f32[3,24,256]{2,1,0:T(8,128)S(1)} %get-tuple-element.17.one_ref), channel_id=1, source_target_pairs={{0,16},{16,0},{1,17},{17,1},{2,18},{18,2},{3,19},{19,3},{4,20},{20... | collective-permute-start | bytes 221192 | tf_op jit(solution)/shard_map/ppermute | solution.py:238
  10.1 5.7 %collective-permute-start.3 = (f32[7,24,128]{2,1,0:T(8,128)S(1)}, f32[7,24,128]{2,1,0:T(8,128)S(1)}, u32[]{:S(2)}, u32[]{:S(2)}) collective-permute-start(f32[7,24,128]{2,1,0:T(8,128)S(1)} %get-tuple-element.22), channel_id=1, source_target_pairs={{0,16},{16,0},{1,17},{17,1},{2,18},{18,2},{3,19},{19,3},{4,20},{20... | collective-permute-start | bytes 258056 | tf_op jit(solution)/shard_map/ppermute | solution.py:243
  10.2 5.6 %collective-permute-start.4 = (f32[2,24,256]{2,1,0:T(8,128)S(1)}, f32[2,24,256]{2,1,0:T(8,128)S(1)}, u32[]{:S(2)}, u32[]{:S(2)}) collective-permute-start(f32[2,24,256]{2,1,0:T(8,128)S(1)} %get-tuple-element.18.field_ref), channel_id=1, source_target_pairs={{0,1},{1,0},{2,3},{3,2},{4,5},{5,4},{6,7},{7,6},{8,9},{9,8},{10,11... | collective-permute-start | bytes 147464 | tf_op jit(solution)/shard_map/ppermute | solution.py:406
  12.2 1.2 %collective-permute-start.1 = (f32[2,1,256]{2,1,0:T(1,128)S(1)}, f32[2,1,256]{2,1,0:T(1,128)S(1)}, u32[]{:S(2)}, u32[]{:S(2)}) collective-permute-start(f32[2,1,256]{2,1,0:T(1,128)S(1)} %get-tuple-element.20), channel_id=1, source_target_pairs={{0,2},{2,0},{4,6},{6,4},{8,10},{10,8},{12,14},{14,12},{1,3},{3,1},... | collective-permute-start | bytes 6152 | tf_op jit(solution)/shard_map/ppermute | solution.py:383
  12.2 3.6 %collective-permute-start.2 = (f32[2,1,256]{2,1,0:T(1,128)S(1)}, f32[2,1,256]{2,1,0:T(1,128)S(1)}, u32[]{:S(2)}, u32[]{:S(2)}) collective-permute-start(f32[2,1,256]{2,1,0:T(1,128)S(1)} %get-tuple-element.21), channel_id=1, source_target_pairs={{2,4},{4,2},{6,8},{8,6},{10,12},{12,10},{3,5},{5,3},{7,9},{9,7},{1... | collective-permute-start | bytes 6152 | tf_op jit(solution)/shard_map/ppermute | solution.py:383
